TPU v7x, 32 devices: a whole 2x2x4 slice. The times are simulated.
32 devices in a mesh: kv: 4 (over z), req: 8 (over y, x, core).
Axes of the slice: x: 2, y: 2, z: 4, core: 2. Of those that a mesh axis runs over, the one named last changes fastest.
Arguments:
- query: bfloat16 [768, 4096], P('req', 'kv'), may hold values from -7 to 7
- latest_key_value: bfloat16 [2, 768, 512], P(None, 'req', 'kv'), may hold values from -5 to 5
- cache: bfloat16 [2, 393216, 512], P(None, 'req', 'kv'), may hold values from -6 to 6
- out_weight: bfloat16 [4096, 4096], P('kv'), may hold values from -0.5 to 0.5
- home: int32 [768], replicated, may hold values from 0 to 767, as said below
- pieces: int32 [2, 768], replicated, may hold values from 0 to 767, as said below
- lengths: int32 [768], replicated, may hold values from 1 to 1920, as said below
Outputs:
- projected: bfloat16 [768, 4096], P('req', 'kv')
Inputs may be any that keep to these rules, and one draw needn't show every extreme that they name: A permutation of the home slots; slot g lies on owner g // 96. The requests i * 96 to (i + 1) * 96 - 1 have their homes on exactly 4 owners, exactly 24 on each. `pieces`: guest slot j lies on owner j // 96. The requests of each index of req have exactly 24 guest slots on each of 4 owners; a request has 4 guest slots or none. Every guest slot has 1 to 384 positions. `lengths`: every home slot gets 1 or more positions, and on every owner the slots take exactly 384 pages.
All inputs are finite; a program needn't handle non-finite values.
Results may differ from a plain program's by a relative error of at most 0.0055.
Values may be sent and summed in bfloat16 or wider, within the bound.
A program may use at most 192 MiB of HBM per device.

v0:
```python
import jax
import jax.numpy as jnp
from jax import lax
from jax.sharding import PartitionSpec as P

QUERY_HEADS = 32
KEY_VALUE_HEADS = 4
HEAD_WIDTH = 128
PAGE_POSITIONS = 128


def rank_in_block(table):
    block_width = table.shape[1]
    same_value = table[:, :, None] == table[:, None, :]
    position = jnp.arange(block_width, dtype=jnp.int32)
    earlier = position[None, :] < position[:, None]
    return jnp.sum((same_value & earlier[None]).astype(jnp.int32), axis=2)


def place_rows(row_keys, slot_total):
    matches = row_keys[None, :] == jnp.arange(slot_total, dtype=jnp.int32)[:, None]
    row_ids = jnp.arange(row_keys.shape[0], dtype=jnp.int32)
    chosen = jnp.sum(jnp.where(matches, row_ids[None, :], 0), axis=1)
    return (chosen, jnp.any(matches, axis=1))


def slot_pages(slot_len, page_count):
    slot_count = slot_len.shape[0]
    per_slot = (slot_len + PAGE_POSITIONS - 1) // PAGE_POSITIONS
    slot_end = jnp.cumsum(per_slot)
    slot_begin = slot_end - per_slot
    page_index = jnp.arange(page_count, dtype=jnp.int32)
    page_slot = jnp.sum((slot_end[None, :] <= page_index[:, None]).astype(jnp.int32), axis=1)
    slot_hot = jnp.arange(slot_count, dtype=jnp.int32)[:, None] == page_slot[None, :]
    page_begin = jnp.sum(jnp.where(slot_hot, slot_begin[:, None], 0), axis=0)
    page_length = jnp.sum(jnp.where(slot_hot, slot_len[:, None], 0), axis=0)
    page_used = jnp.clip(
        page_length - (page_index - page_begin) * PAGE_POSITIONS, 0, PAGE_POSITIONS
    )
    return (page_slot, slot_hot, page_used)


def local_attention(slot_query, slot_len, cache, kv_local, group_width):
    page_count = cache.shape[1] // PAGE_POSITIONS
    head_count = kv_local * group_width
    page_slot, slot_hot, page_used = slot_pages(slot_len, page_count)
    page_query = jnp.take(slot_query, page_slot, axis=0).reshape(
        page_count, kv_local, group_width, HEAD_WIDTH
    )
    page_keys = cache[0].reshape(page_count, PAGE_POSITIONS, kv_local, HEAD_WIDTH)
    page_values = cache[1].reshape(page_count, PAGE_POSITIONS, kv_local, HEAD_WIDTH)
    scores = jnp.einsum(
        "pkgd,ptkd->pkgt", page_query, page_keys, preferred_element_type=jnp.float32
    ) * HEAD_WIDTH ** (-0.5)
    in_use = (jnp.arange(PAGE_POSITIONS, dtype=jnp.int32)[None, :] < page_used[:, None])[
        :, None, None, :
    ]
    scores = jnp.where(in_use, scores, -jnp.inf)
    page_top = jnp.max(scores, axis=-1).reshape(page_count, head_count)
    slot_maximum = jnp.max(jnp.where(slot_hot[:, :, None], page_top[None, :, :], -jnp.inf), axis=1)
    shifted = scores - jnp.take(slot_maximum, page_slot, axis=0).reshape(
        page_count, kv_local, group_width, 1
    )
    weights = jnp.where(in_use, jnp.exp(shifted), 0.0).astype(jnp.bfloat16)
    hot_float = slot_hot.astype(jnp.float32)
    page_sum = jnp.sum(weights, axis=-1, dtype=jnp.float32).reshape(page_count, head_count)
    slot_total_sum = jnp.dot(hot_float, page_sum, precision=lax.Precision.HIGHEST)
    page_out = jnp.einsum(
        "pkgt,ptkd->pkgd", weights, page_values, preferred_element_type=jnp.float32
    )
    slot_out = jnp.dot(
        hot_float,
        page_out.reshape(page_count, head_count * HEAD_WIDTH),
        precision=lax.Precision.HIGHEST,
    )
    slot_average = (
        slot_out.reshape(-1, head_count, HEAD_WIDTH) / slot_total_sum[:, :, None]
    ).astype(jnp.bfloat16)
    return (slot_maximum, slot_total_sum, slot_average.reshape(-1, head_count * HEAD_WIDTH))


def per_device(query, latest_key_value, cache, out_weight, home, pieces, lengths):
    req_count = lax.axis_size("req")
    device_index = lax.axis_index("req")
    row_count = query.shape[0]
    q_width = query.shape[1]
    batch_size = home.shape[0]
    extra_count = pieces.shape[1] // req_count
    home_cap = 2 * row_count // req_count
    piece_cap = 2 * extra_count // req_count
    group_width = QUERY_HEADS // KEY_VALUE_HEADS
    kv_local = latest_key_value.shape[2] // HEAD_WIDTH
    head_count = kv_local * group_width
    dest_all = home // row_count
    home_rank = rank_in_block(dest_all.reshape(req_count, row_count)).reshape(batch_size)
    piece_req = pieces[0]
    piece_len = pieces[1]
    piece_src = piece_req // row_count
    piece_rank = rank_in_block(piece_src.reshape(req_count, extra_count)).reshape(
        req_count * extra_count
    )
    my_dest = lax.dynamic_slice_in_dim(dest_all, device_index * row_count, row_count)
    my_rank = lax.dynamic_slice_in_dim(home_rank, device_index * row_count, row_count)
    mine_at = my_dest * home_cap + my_rank
    home_row, home_live = place_rows(mine_at, req_count * home_cap)
    home_rows_sent = jnp.take(query, home_row, axis=0)
    home_buf = jnp.where(home_live[:, None], home_rows_sent, jnp.zeros_like(home_rows_sent))
    home_buf = home_buf.reshape(req_count, home_cap, q_width)
    owner_of = jnp.arange(req_count * extra_count, dtype=jnp.int32) // extra_count
    piece_key = jnp.where(piece_src == device_index, owner_of * piece_cap + piece_rank, -1)
    piece_pick, piece_live = place_rows(piece_key, req_count * piece_cap)
    piece_row = jnp.clip(
        jnp.take(piece_req, piece_pick) - device_index * row_count, 0, row_count - 1
    )
    my_slots = device_index * row_count + jnp.arange(row_count, dtype=jnp.int32)
    own_hot = home[None, :] == my_slots[:, None]
    home_req = jnp.sum(
        jnp.where(own_hot, jnp.arange(batch_size, dtype=jnp.int32)[None, :], 0), axis=1
    )
    home_at = home_req // row_count * home_cap + jnp.take(home_rank, home_req)
    guest_req = lax.dynamic_slice_in_dim(piece_req, device_index * extra_count, extra_count)
    guest_len = lax.dynamic_slice_in_dim(piece_len, device_index * extra_count, extra_count)
    guest_src = lax.dynamic_slice_in_dim(piece_src, device_index * extra_count, extra_count)
    guest_rank = lax.dynamic_slice_in_dim(piece_rank, device_index * extra_count, extra_count)
    guest_at = guest_src * piece_cap + guest_rank
    guest_total = jnp.sum(
        jnp.where(home_req[:, None] == piece_req[None, :], piece_len[None, :], 0), axis=1
    )
    home_len = jnp.take(lengths, home_req) - guest_total
    slot_len = jnp.concatenate([home_len, guest_len])
    everyone = lax.all_gather(query, "req", axis=0, tiled=True)
    arrived = lax.all_to_all(home_buf, "req", split_axis=0, concat_axis=0, tiled=True)
    guest_query = jnp.take(everyone, guest_req, axis=0)
    home_query = jnp.take(arrived.reshape(req_count * home_cap, q_width), home_at, axis=0)
    slot_query = jnp.concatenate([home_query, guest_query], axis=0)
    slot_maximum, slot_total_sum, slot_average = local_attention(
        slot_query, slot_len, cache, kv_local, group_width
    )
    back_home, home_full = place_rows(home_at, req_count * home_cap)
    back_piece, piece_full = place_rows(guest_at, req_count * piece_cap)
    home_shape = (req_count, home_cap)
    piece_shape = (req_count, piece_cap)
    send_home_top = jnp.take(slot_maximum[:row_count], back_home, axis=0).reshape(
        home_shape + (head_count,)
    )
    send_home_sum = jnp.take(slot_total_sum[:row_count], back_home, axis=0).reshape(
        home_shape + (head_count,)
    )
    send_home_avg = jnp.take(slot_average[:row_count], back_home, axis=0).reshape(
        home_shape + (head_count * HEAD_WIDTH,)
    )
    send_piece_top = jnp.take(slot_maximum[row_count:], back_piece, axis=0).reshape(
        piece_shape + (head_count,)
    )
    send_piece_sum = jnp.take(slot_total_sum[row_count:], back_piece, axis=0).reshape(
        piece_shape + (head_count,)
    )
    send_piece_avg = jnp.take(slot_average[row_count:], back_piece, axis=0).reshape(
        piece_shape + (head_count * HEAD_WIDTH,)
    )
    got_home_top, got_home_sum, got_piece_top, got_piece_sum = (
        lax.all_to_all(send_home_top, "req", split_axis=0, concat_axis=0, tiled=True),
        lax.all_to_all(send_home_sum, "req", split_axis=0, concat_axis=0, tiled=True),
        lax.all_to_all(send_piece_top, "req", split_axis=0, concat_axis=0, tiled=True),
        lax.all_to_all(send_piece_sum, "req", split_axis=0, concat_axis=0, tiled=True),
    )
    got_home_avg, got_piece_avg = (
        lax.all_to_all(send_home_avg, "req", split_axis=0, concat_axis=0, tiled=True),
        lax.all_to_all(send_piece_avg, "req", split_axis=0, concat_axis=0, tiled=True),
    )
    home_top = jnp.take(got_home_top.reshape(-1, head_count), mine_at, axis=0)
    home_sum = jnp.take(got_home_sum.reshape(-1, head_count), mine_at, axis=0)
    home_avg = jnp.take(got_home_avg.reshape(-1, head_count * HEAD_WIDTH), mine_at, axis=0)
    home_avg = home_avg.astype(jnp.float32).reshape(row_count, head_count, HEAD_WIDTH)
    piece_top = got_piece_top.reshape(-1, head_count)
    piece_sum = got_piece_sum.reshape(-1, head_count)
    piece_avg = got_piece_avg.reshape(-1, head_count, HEAD_WIDTH).astype(jnp.float32)
    query_heads = query.reshape(row_count, kv_local, group_width, HEAD_WIDTH)
    latest_keys = latest_key_value[0].reshape(row_count, kv_local, HEAD_WIDTH)
    self_score = jnp.einsum(
        "rkgd,rkd->rkg", query_heads, latest_keys, preferred_element_type=jnp.float32
    )
    self_score = self_score.reshape(row_count, head_count) * HEAD_WIDTH ** (-0.5)
    latest_values = jnp.broadcast_to(
        latest_key_value[1].astype(jnp.float32).reshape(row_count, kv_local, 1, HEAD_WIDTH),
        (row_count, kv_local, group_width, HEAD_WIDTH),
    ).reshape(row_count, head_count, HEAD_WIDTH)
    guest_hot = (
        piece_row[None, :] == jnp.arange(row_count, dtype=jnp.int32)[:, None]
    ) & piece_live[None, :]
    guest_best = jnp.max(jnp.where(guest_hot[:, :, None], piece_top[None, :, :], -jnp.inf), axis=1)
    row_top = jnp.maximum(jnp.maximum(home_top, self_score), guest_best)
    home_coef = home_sum * jnp.exp(home_top - row_top)
    own_factor = jnp.exp(self_score - row_top)
    piece_coef = jnp.where(
        piece_live[:, None],
        piece_sum * jnp.exp(piece_top - jnp.take(row_top, piece_row, axis=0)),
        0.0,
    )
    hot_float = guest_hot.astype(jnp.float32)
    denominator = home_coef + own_factor
    denominator = denominator + jnp.dot(hot_float, piece_coef, precision=lax.Precision.HIGHEST)
    weighted_piece = (piece_avg * piece_coef[:, :, None]).reshape(-1, head_count * HEAD_WIDTH)
    numerator = home_avg * home_coef[:, :, None] + latest_values * own_factor[:, :, None]
    numerator = numerator + jnp.dot(
        hot_float, weighted_piece, precision=lax.Precision.HIGHEST
    ).reshape(row_count, head_count, HEAD_WIDTH)
    attended = (
        (numerator / denominator[:, :, None]).astype(jnp.bfloat16).reshape(row_count, q_width)
    )
    projected = jnp.dot(attended, out_weight, preferred_element_type=jnp.float32)
    return lax.psum_scatter(projected, "kv", scatter_dimension=1, tiled=True).astype(jnp.bfloat16)


def solution(mesh):
    placed = (
        P("req", "kv"),
        P(None, "req", "kv"),
        P(None, "req", "kv"),
        P("kv", None),
        P(),
        P(),
        P(),
    )
    return jax.shard_map(
        per_device, mesh=mesh, in_specs=placed, out_specs=P("req", "kv"), check_vma=False
    )
```

profile of v0, /device:TPU:0, one launch (start us, length us, event | category | flops | bytes accessed | tf_op | source)
XLA Modules:
  0.0 181.9 jit_solution(660537088172356555)
XLA Ops:
  6.5 0.7 all-gather.2.cloned.1.call-update
  7.3 0.7 fusion.38
  8.0 0.7 fusion.34
  8.9 0.7 add_select_fusion.2
  9.7 0.6 convert_reduce_fusion.1
  10.3 0.6 compare_and_fusion.3
  11.2 1.0 gather_fusion.5
  12.2 0.9 select_select_fusion
  13.1 5.2 %all-to-all-start = ((bf16[8,24,1024]{2,1,0:T(8,128)(2,1)}), bf16[8,24,1024]{2,1,0:T(8,128)(2,1)S(1)}, u32[]{:S(2)}, u32[]{:S(2)}) async-start(bf16[8,24,1024]{2,1,0:T(8,128)(2,1)} %bitcast.4), calls=%async_computation | async-start | bytes 786432 | tf_op jit(solution)/shard_map/all_to_all | solution.py:132
  18.5 1.0 gather_fusion.6
  20.4 1.0 gather_fusion.4
  22.5 17.0 %fusion.39 = (bf16[1,49152,128]{2,1,0:T(8,128)(2,1)}, bf16[1,49152,128]{2,1,0:T(8,128)(2,1)}) fusion(bf16[2,49152,128]{2,1,0:T(8,128)(2,1)} %param.19), kind=kLoop, calls=%fused_computation.177 | loop fusion | bytes 50331648 | tf_op jit(solution)/shard_map/slice | solution.py:51
  39.5 0.6 pad_clamp_fusion.3
  40.5 1.2 gather_fusion.3
  41.7 0.5 compare_and_fusion.2
  42.2 0.5 compare_and_fusion.1
  43.3 0.6 pad_clamp_fusion
  44.0 0.8 gather_fusion.7
  44.9 2.5 %gather_fusion = bf16[96,1024]{1,0:T(8,128)(2,1)S(1)} fusion(bf16[768,1024]{1,0:T(8,128)(2,1)} %all-gather.2.cloned.1.call-done, s32[1024]{0:T(1024)S(1)} %pad_clamp_fusion.6), kind=kCustom, calls=%fused_computation.14 | custom fusion | bytes 393600 | tf_op jit(solution)/shard_map/jit(_take)/gather | solution.py:133
  47.5 2.1 %gather_fusion.1 = bf16[384,1024]{1,0:T(8,128)(2,1)S(1)} fusion(bf16[192,1024]{1,0:T(8,128)(2,1)S(1)} %pad_maximum_fusion, s32[1024]{0:T(1024)S(1)} %pad_clamp_fusion.5), kind=kCustom, calls=%fused_computation.15 | custom fusion | bytes 1574400 | tf_op jit(solution)/shard_map/jit(_take)/gather | solution.py:47
  49.8 1.3 bitcast_select_fusion
  51.1 9.3 %fusion.42 = (f32[384,8]{1,0:T(8,128)S(1)}, f32[384,8,128]{2,1,0:T(8,128)S(1)}) fusion(bf16[384,8,128]{2,1,0:T(8,128)(2,1)S(1)} %bitcast_select_fusion, bf16[384,128,128]{2,1,0:T(8,128)(2,1)} %bitcast.119, pred[384,128]{1,0:T(8,128)(4,1)S(1)} %iota_compare_fusion.4), kind=kOutput, calls=%fused_computation.180 | convolution fusion | flops 101839872 | bytes 15003648 | tf_op jit(solution)/shard_map/pkgd,ptkd->pkgt/dot_general | solution.py:52
  60.9 1.1 gather_fusion.2
  62.2 1.0 convert_reduce_fusion
  63.7 0.7 gather_fusion.10
  64.4 0.7 gather_fusion.12
  65.3 0.7 reshape.714
  66.0 4.2 %all-to-all-start.2 = ((f32[8,1,192]{2,1,0:T(1,128)}), f32[8,1,192]{2,1,0:T(1,128)S(1)}, u32[]{:S(2)}, u32[]{:S(2)}) async-start(f32[8,1,192]{2,1,0:T(1,128)} %reshape.714), calls=%async_computation.2 | async-start | bytes 16384 | tf_op jit(solution)/shard_map/all_to_all | solution.py:163
  70.2 0.7 gather_fusion.16
  70.9 0.7 gather_fusion.14
  71.6 6.9 %fusion.33 = f32[384,8,128]{2,1,0:T(8,128)S(1)} fusion(bf16[384,128,128]{2,1,0:T(8,128)(2,1)} %bitcast.118, f32[384,8,128]{2,1,0:T(8,128)S(1)} %get-tuple-element.48, f32[384,8]{1,0:T(8,128)S(1)} %broadcast_select_fusion.4, pred[384,128]{1,0:T(8,128)(4,1)S(1)} %iota_compare_fusion.4), kind=kOutput, calls=%fused_computation.174 | convolution fusion | flops 101842944 | bytes 15790080 | tf_op jit(solution)/shard_map/pkgt,ptkd->pkgd/dot_general | solution.py:68
  78.9 0.5 copy.66
  79.4 1.1 fusion
  80.6 0.6 copy-done.10
  81.3 0.7 reshape.710
  82.0 1.0 gather_fusion.15
  83.0 4.2 %all-to-all-start.4 = ((f32[8,1,192]{2,1,0:T(1,128)}), f32[8,1,192]{2,1,0:T(1,128)S(1)}, u32[]{:S(2)}, u32[]{:S(2)}) async-start(f32[8,1,192]{2,1,0:T(1,128)} %reshape.710), calls=%async_computation.4 | async-start | bytes 16384 | tf_op jit(solution)/shard_map/all_to_all | solution.py:164
  87.3 0.8 broadcast_select_fusion
  88.2 0.7 reshape.712
  88.9 1.0 gather_fusion.8
  89.9 2.1 %all-to-all-done.4 = f32[8,1,192]{2,1,0:T(1,128)S(1)} async-done(((f32[8,1,192]{2,1,0:T(1,128)}), f32[8,1,192]{2,1,0:T(1,128)S(1)}, u32[]{:S(2)}, u32[]{:S(2)}) %all-to-all-start.4) | async-done | bytes 6176 | tf_op jit(solution)/shard_map/all_to_all | solution.py:164
  92.0 3.3 %all-to-all-start.3 = ((f32[8,1,192]{2,1,0:T(1,128)}), f32[8,1,192]{2,1,0:T(1,128)S(1)}, u32[]{:S(2)}, u32[]{:S(2)}) async-start(f32[8,1,192]{2,1,0:T(1,128)} %reshape.712), calls=%async_computation.3 | async-start | bytes 16384 | tf_op jit(solution)/shard_map/all_to_all | solution.py:162
  95.3 0.9 broadcast_select_fusion.1
  96.2 0.7 reshape.708
  96.9 0.5 broadcast.440
  97.4 0.6 reduce.19
  98.2 1.7 all-to-all-done.3
  99.9 3.3 %all-to-all-start.6 = ((f32[8,1,192]{2,1,0:T(1,128)}), f32[8,1,192]{2,1,0:T(1,128)S(1)}, u32[]{:S(2)}, u32[]{:S(2)}) async-start(f32[8,1,192]{2,1,0:T(1,128)} %reshape.708), calls=%async_computation.6 | async-start | bytes 16384 | tf_op jit(solution)/shard_map/all_to_all | solution.py:165
  103.5 0.6 reduce.20
  104.2 0.7 gather_fusion.13
  105.1 2.8 %all-to-all-done.6 = f32[8,1,192]{2,1,0:T(1,128)S(1)} async-done(((f32[8,1,192]{2,1,0:T(1,128)}), f32[8,1,192]{2,1,0:T(1,128)S(1)}, u32[]{:S(2)}, u32[]{:S(2)}) %all-to-all-start.6) | async-done | bytes 6176 | tf_op jit(solution)/shard_map/all_to_all | solution.py:165
  107.9 3.5 %all-to-all-start.1 = ((bf16[8,24,1024]{2,1,0:T(8,128)(2,1)}), bf16[8,24,1024]{2,1,0:T(8,128)(2,1)S(1)}, u32[]{:S(2)}, u32[]{:S(2)}) async-start(bf16[8,24,1024]{2,1,0:T(8,128)(2,1)} %bitcast.13), calls=%async_computation.1 | async-start | bytes 786432 | tf_op jit(solution)/shard_map/all_to_all | solution.py:168
  111.4 0.6 reduce.21
  112.1 0.7 gather_fusion.11
  113.0 0.6 reduce.18
  113.8 0.8 gather_fusion.17
  114.8 4.9 %all-to-all-done.1 = bf16[8,24,1024]{2,1,0:T(8,128)(2,1)S(1)} async-done(((bf16[8,24,1024]{2,1,0:T(8,128)(2,1)}), bf16[8,24,1024]{2,1,0:T(8,128)(2,1)S(1)}, u32[]{:S(2)}, u32[]{:S(2)}) %all-to-all-start.1) | async-done | bytes 393248 | tf_op jit(solution)/shard_map/all_to_all | solution.py:168
  119.6 3.5 %all-to-all-start.5 = ((bf16[8,24,1024]{2,1,0:T(8,128)(2,1)}), bf16[8,24,1024]{2,1,0:T(8,128)(2,1)S(1)}, u32[]{:S(2)}, u32[]{:S(2)}) async-start(bf16[8,24,1024]{2,1,0:T(8,128)(2,1)} %bitcast.28), calls=%async_computation.5 | async-start | bytes 786432 | tf_op jit(solution)/shard_map/all_to_all | solution.py:169
  123.4 0.9 gather_fusion.9
  124.3 7.1 %all-to-all-done.5 = bf16[8,24,1024]{2,1,0:T(8,128)(2,1)S(1)} async-done(((bf16[8,24,1024]{2,1,0:T(8,128)(2,1)}), bf16[8,24,1024]{2,1,0:T(8,128)(2,1)S(1)}, u32[]{:S(2)}, u32[]{:S(2)}) %all-to-all-start.5) | async-done | bytes 393248 | tf_op jit(solution)/shard_map/all_to_all | solution.py:169
  131.9 0.6 fusion.3
  132.5 6.0 %fusion.12 = f32[96,4096]{1,0:T(8,128)} fusion(bf16[1024,4096]{1,0:T(8,128)(2,1)} %param.20, bf16[8,12,8,128]{3,2,1,0:T(8,128)(2,1)S(1)} %fusion.3), kind=kOutput, calls=%fused_computation.57 | convolution fusion | flops 805306368 | bytes 10158080 | tf_op jit(solution)/shard_map/dot_general | solution.py:211
  138.5 34.8 %reduce-scatter.2.cloned.1.call-done = f32[96,1024]{1,0:T(8,128)} async-done(((f32[96,4096]{1,0:T(8,128)}), f32[96,1024]{1,0:T(8,128)}) %reduce-scatter.2.cloned.1.call-update) | async-done | bytes 393232 | tf_op jit(solution)/shard_map/reduce_scatter | solution.py:212
  173.4 1.7 convert_element_type.57
  (131 shorter events, 8.3 us)
Async XLA Ops:
  6.5 13.9 %copy-start = (s32[768]{0:T(1024)S(1)}, s32[768]{0:T(1024)}, u32[]{:S(2)}) copy-start(s32[768]{0:T(1024)} %param.23) | copy-start | bytes 9220
  6.5 4.7 %copy-start.2 = (bf16[96,1024]{1,0:T(8,128)(2,1)S(1)}, bf16[96,1024]{1,0:T(8,128)(2,1)}, u32[]{:S(2)}) copy-start(bf16[96,1024]{1,0:T(8,128)(2,1)} %param.17) | copy-start | bytes 589828
  6.5 38.3 %all-gather.2.cloned.1.call-start = ((), (), s32[]{:S(2)}) async-start(), calls=%async_computation.8 | async-start | bytes 1769472 | tf_op jit(solution)/shard_map/all_gather | solution.py:131
  12.2 6.1 %copy-start.5 = (s32[768]{0:T(1024)S(1)}, s32[768]{0:T(1024)}, u32[]{:S(2)}) copy-start(s32[768]{0:T(1024)} %param.21) | copy-start | bytes 9220
  12.2 7.6 %copy-start.4 = (s32[2,768]{1,0:T(2,128)S(1)}, s32[2,768]{1,0:T(2,128)}, u32[]{:S(2)}) copy-start(s32[2,768]{1,0:T(2,128)} %param.22) | copy-start | bytes 18436
  13.1 30.8 %all-to-all-start = ((bf16[8,24,1024]{2,1,0:T(8,128)(2,1)}), bf16[8,24,1024]{2,1,0:T(8,128)(2,1)S(1)}, u32[]{:S(2)}, u32[]{:S(2)}) async-start(bf16[8,24,1024]{2,1,0:T(8,128)(2,1)} %bitcast.4), calls=%async_computation | async-start | bytes 786432 | tf_op jit(solution)/shard_map/all_to_all | solution.py:132
  19.7 45.4 %copy-start.8 = (pred[192]{0:T(512)(128)(4,1)}, pred[192]{0:T(512)(128)(4,1)S(1)}, u32[]{:S(2)}) copy-start(pred[192]{0:T(512)(128)(4,1)S(1)} %compare_and_fusion.4) | copy-start | bytes 580
  39.5 3.4 %copy-start.3 = (bf16[2,96,128]{2,1,0:T(8,128)(2,1)S(1)}, bf16[2,96,128]{2,1,0:T(8,128)(2,1)}, u32[]{:S(2)}) copy-start(bf16[2,96,128]{2,1,0:T(8,128)(2,1)} %param.18) | copy-start | bytes 147460
  66.0 17.1 %all-to-all-start.2 = ((f32[8,1,192]{2,1,0:T(1,128)}), f32[8,1,192]{2,1,0:T(1,128)S(1)}, u32[]{:S(2)}, u32[]{:S(2)}) async-start(f32[8,1,192]{2,1,0:T(1,128)} %reshape.714), calls=%async_computation.2 | async-start | bytes 16384 | tf_op jit(solution)/shard_map/all_to_all | solution.py:163
  80.5 0.7 copy-start.10
  83.0 8.9 %all-to-all-start.4 = ((f32[8,1,192]{2,1,0:T(1,128)}), f32[8,1,192]{2,1,0:T(1,128)S(1)}, u32[]{:S(2)}, u32[]{:S(2)}) async-start(f32[8,1,192]{2,1,0:T(1,128)} %reshape.710), calls=%async_computation.4 | async-start | bytes 16384 | tf_op jit(solution)/shard_map/all_to_all | solution.py:164
  88.9 6.4 %copy-start.9 = (pred[192]{0:T(512)(128)(4,1)S(1)}, pred[192]{0:T(512)(128)(4,1)}, u32[]{:S(2)}) copy-start(pred[192]{0:T(512)(128)(4,1)} %copy-done.8) | copy-start | bytes 580
  89.9 21.5 %copy-start.6 = (pred[96]{0:T(512)(128)(4,1)S(1)}, pred[96]{0:T(512)(128)(4,1)}, u32[]{:S(2)}) copy-start(pred[96]{0:T(512)(128)(4,1)} %get-tuple-element.21) | copy-start | bytes 292
  92.0 8.0 %all-to-all-start.3 = ((f32[8,1,192]{2,1,0:T(1,128)}), f32[8,1,192]{2,1,0:T(1,128)S(1)}, u32[]{:S(2)}, u32[]{:S(2)}) async-start(f32[8,1,192]{2,1,0:T(1,128)} %reshape.712), calls=%async_computation.3 | async-start | bytes 16384 | tf_op jit(solution)/shard_map/all_to_all | solution.py:162
  99.9 8.0 %all-to-all-start.6 = ((f32[8,1,192]{2,1,0:T(1,128)}), f32[8,1,192]{2,1,0:T(1,128)S(1)}, u32[]{:S(2)}, u32[]{:S(2)}) async-start(f32[8,1,192]{2,1,0:T(1,128)} %reshape.708), calls=%async_computation.6 | async-start | bytes 16384 | tf_op jit(solution)/shard_map/all_to_all | solution.py:165
  104.2 10.4 %copy-start.7 = (pred[192]{0:T(512)(128)(4,1)S(1)}, pred[192]{0:T(512)(128)(4,1)}, u32[]{:S(2)}) copy-start(pred[192]{0:T(512)(128)(4,1)} %get-tuple-element.19) | copy-start | bytes 580
  107.9 11.7 %all-to-all-start.1 = ((bf16[8,24,1024]{2,1,0:T(8,128)(2,1)}), bf16[8,24,1024]{2,1,0:T(8,128)(2,1)S(1)}, u32[]{:S(2)}, u32[]{:S(2)}) async-start(bf16[8,24,1024]{2,1,0:T(8,128)(2,1)} %bitcast.13), calls=%async_computation.1 | async-start | bytes 786432 | tf_op jit(solution)/shard_map/all_to_all | solution.py:168
  119.6 11.7 %all-to-all-start.5 = ((bf16[8,24,1024]{2,1,0:T(8,128)(2,1)}), bf16[8,24,1024]{2,1,0:T(8,128)(2,1)S(1)}, u32[]{:S(2)}, u32[]{:S(2)}) async-start(bf16[8,24,1024]{2,1,0:T(8,128)(2,1)} %bitcast.28), calls=%async_computation.5 | async-start | bytes 786432 | tf_op jit(solution)/shard_map/all_to_all | solution.py:169
  123.1 50.3 %reduce-scatter.2.cloned.1.call-start = ((), (), s32[]{:S(2)}) async-start(), calls=%async_computation.9 | async-start | bytes 1966080 | tf_op jit(solution)/shard_map/reduce_scatter | solution.py:212
  132.4 42.6 %copy-start.1 = (s32[768]{0:T(1024)S(1)}, s32[768]{0:T(1024)}, u32[]{:S(2)}) copy-start(s32[768]{0:T(1024)} %param.23) | copy-start | bytes 9220
Sparse Core Ops, SparseCore 0:
  9.2 32.3 all-gather.1
  138.7 34.6 reduce-scatter.1
where the time goes:
time: 183 us; the launch traced here: 182 us
  waiting for transfers between devices  54.1 us (30%)
  local copies, waits for them, and re-layouts  43.4 us (24%)
  starting transfers between devices  27.2 us (15%)
  matrix products  24.7 us (13%)
  other arithmetic  18.5 us (10%)
  between operations  14.1 us (8%)
    reduce_scatter x1, waiting for transfers between devices, per_device(): lax.psum_scatter(projected, 'kv', scatter_dimension=1, tiled=True)  34.8 us
    slice x1, local copies, waits for them, and re-layouts, local_attention(): cache[1].reshape(page_count, PAGE_POSITIONS, kv_local, HEAD_WIDTH)  17 us
    dot_general x1, matrix products, local_attention(): jnp.einsum('pkgd,ptkd->pkgt', page_query, page_keys, preferred_element_ty...  9.27 us
    all_to_all x1, waiting for transfers between devices, per_device(): lax.all_to_all(send_piece_avg, 'req', split_axis=0, concat_axis=0, tiled=...  7.06 us
    dot_general x1, matrix products, local_attention(): jnp.einsum('pkgt,ptkd->pkgd', weights, page_values, preferred_element_typ...  6.91 us
    dot_general x1, matrix products, per_device(): jnp.dot(attended, out_weight, preferred_element_type=jnp.float32)  6.05 us
    all_to_all x1, starting transfers between devices, per_device(): lax.all_to_all(home_buf, 'req', split_axis=0, concat_axis=0, tiled=True)  5.17 us
    all_to_all x1, waiting for transfers between devices, per_device(): lax.all_to_all(send_home_avg, 'req', split_axis=0, concat_axis=0, tiled=T...  4.87 us
  transfers between devices with their start and end apart: 9, of which 6 were waited for; matrix products, arithmetic and copies ran while one was open for 31% of the time, Pallas kernels for 0%

commit v1 on v0

v1 whole, which is shorter than its diff:
```python
import functools

import jax
import jax.numpy as jnp
from jax import lax
from jax.experimental import pallas as pl
from jax.experimental.pallas import tpu as pltpu
from jax.sharding import PartitionSpec as P

QUERY_HEADS = 32
KEY_VALUE_HEADS = 4
HEAD_WIDTH = 128
PAGE_POSITIONS = 128
MAX_SLOT_PAGES = 15
GROUP = QUERY_HEADS // KEY_VALUE_HEADS
PAGE_BLOCK = 32
STATS = 128
NT = (((1,), (1,)), ((), ()))
NEG = float("-inf")
MESH = pl.DeviceIdType.MESH


def tables(home, pieces, lengths, me, req_count, rows, extra, page_count):
    home_cap = 2 * rows // req_count
    piece_cap = 2 * extra // req_count
    entries = -(-(home_cap + piece_cap) // 16) * 16
    total = req_count * entries
    i32 = jnp.int32
    batch = home.shape[0]
    dest = home // rows
    request = jnp.arange(batch, dtype=i32)

    def rank(table):
        width = table.shape[1]
        at = jnp.arange(width, dtype=i32)
        earlier = at[None, :] < at[:, None]
        same = table[:, :, None] == table[:, None, :]
        return jnp.sum((same & earlier[None]).astype(i32), axis=2).reshape(-1)

    home_rank = rank(dest.reshape(req_count, rows))
    piece_req, piece_len = pieces[0], pieces[1]
    piece_src = piece_req // rows
    piece_rank = rank(piece_src.reshape(req_count, extra)) + home_cap
    piece_owner = jnp.arange(req_count * extra, dtype=i32) // extra
    entry = jnp.arange(total, dtype=i32)[:, None]
    home_key = jnp.where(request // rows == me, dest * entries + home_rank, -1)
    piece_key = jnp.where(piece_src == me, piece_owner * entries + piece_rank, -1)
    keys = jnp.concatenate([home_key, piece_key])
    key_rows = jnp.concatenate([request, piece_req]) - me * rows + 1
    row_of_entry = jnp.sum(jnp.where(keys[None, :] == entry, key_rows[None, :], 0), axis=1) - 1
    my_slots = me * rows + jnp.arange(rows, dtype=i32)
    hot = home[None, :] == my_slots[:, None]
    at_home = jnp.sum(jnp.where(hot, (request // rows * entries + home_rank)[None, :], 0), axis=1)
    moved = jnp.sum(
        jnp.where(request[:, None] == piece_req[None, :], piece_len[None, :], 0), axis=1
    )
    home_len = jnp.sum(jnp.where(hot, (lengths - moved)[None, :], 0), axis=1)
    guest_at = lax.dynamic_slice_in_dim(piece_src * entries + piece_rank, me * extra, extra)
    guest_len = lax.dynamic_slice_in_dim(piece_len, me * extra, extra)
    slot_at = jnp.concatenate([at_home, guest_at])
    slot_len = jnp.concatenate([home_len, guest_len])
    per_slot = (slot_len + PAGE_POSITIONS - 1) // PAGE_POSITIONS
    slot = jnp.arange(rows + extra, dtype=i32)
    begin = jnp.sum(jnp.where(slot[None, :] < slot[:, None], per_slot[None, :], 0), axis=1)
    page = jnp.arange(page_count, dtype=i32)[:, None]
    held = (begin[None, :] <= page) & (page < (begin + per_slot)[None, :])
    page_at = jnp.sum(jnp.where(held, slot_at[None, :], 0), axis=1)
    left = slot_len[None, :] - (page - begin[None, :]) * PAGE_POSITIONS
    page_used = jnp.sum(jnp.where(held, jnp.clip(left, 0, PAGE_POSITIONS), 0), axis=1)
    page_first = jnp.sum((held & (page == begin[None, :])).astype(i32), axis=1)
    return entries, row_of_entry, page_at, page_used, page_first


def greet(axis, n):
    me = lax.axis_index(axis)
    barrier = pltpu.get_barrier_semaphore()
    for step in range(1, n):
        peer = lax.rem(me + step, n)
        pl.semaphore_signal(barrier, inc=1, device_id={axis: peer}, device_id_type=MESH)
    return barrier


def send_kernel(n, entries, row_ref, query_ref, out_ref, packed, send_sem, recv_sem, own_sem):
    me = lax.axis_index("req")
    barrier = greet("req", n)
    rows = query_ref.shape[0]
    pick = row_ref[...] == lax.broadcasted_iota(jnp.int32, (n * entries, rows), 1)
    pick = jnp.where(pick, 1.0, 0.0).astype(jnp.bfloat16)
    width = query_ref.shape[1]
    packed[...] = (
        jnp.dot(pick, query_ref[...], preferred_element_type=jnp.float32)
        .astype(jnp.bfloat16)
        .reshape(n, entries, width)
    )
    own = pltpu.make_async_copy(packed.at[me], out_ref.at[me], own_sem)
    own.start()
    pl.semaphore_wait(barrier, n - 1)
    copies = []
    for step in range(1, n):
        peer = lax.rem(me + step, n)
        copy = pltpu.make_async_remote_copy(
            src_ref=packed.at[peer],
            dst_ref=out_ref.at[me],
            send_sem=send_sem.at[step],
            recv_sem=recv_sem.at[step],
            device_id={"req": peer},
            device_id_type=MESH,
        )
        copy.start()
        copies.append(copy)
    own.wait()
    for copy in copies:
        copy.wait()


def segment_scan(x, at, lane, width, combine, empty):
    ahead, behind = x, x
    shift = 1
    while shift < MAX_SLOT_PAGES:
        same = (pltpu.roll(at, shift, 1) == at) & (lane >= shift)
        ahead = combine(ahead, jnp.where(same, pltpu.roll(ahead, shift, 1), empty))
        same = (pltpu.roll(at, width - shift, 1) == at) & (lane < width - shift)
        behind = combine(behind, jnp.where(same, pltpu.roll(behind, width - shift, 1), empty))
        shift *= 2
    return ahead, behind


def attention_kernel(
    used_ref, col_ref, row_ref, first_ref, arrived_ref, key_ref, value_ref,
    out_ref, q_buf, o_buf, top_buf, sum_buf,
):
    step = pl.program_id(0)
    pages = col_ref.shape[0]
    total = arrived_ref.shape[0]
    scale = HEAD_WIDTH ** (-0.5)

    @pl.when(step == 0)
    def _():
        hot = col_ref[...] == lax.broadcasted_iota(jnp.int32, (pages, total), 1)
        hot = jnp.where(hot, 1.0, 0.0).astype(jnp.bfloat16)
        for h in range(GROUP):
            q_buf[pl.ds(h, pages, stride=GROUP), :] = jnp.dot(
                hot,
                arrived_ref[:, h * HEAD_WIDTH : (h + 1) * HEAD_WIDTH],
                preferred_element_type=jnp.float32,
            )

    lane = lax.broadcasted_iota(jnp.int32, (GROUP, 128), 1)
    per_chunk = 128 // PAGE_BLOCK
    lane0 = lax.rem(step, per_chunk) * PAGE_BLOCK
    chunk = step // per_chunk
    tops = top_buf[chunk]
    sums = sum_buf[chunk]
    for j in range(PAGE_BLOCK):
        p = step * PAGE_BLOCK + j
        q = q_buf[pl.ds(pl.multiple_of(p * GROUP, GROUP), GROUP), :].astype(jnp.bfloat16)
        keys = key_ref[0, j * PAGE_POSITIONS : (j + 1) * PAGE_POSITIONS, :]
        values = value_ref[0, j * PAGE_POSITIONS : (j + 1) * PAGE_POSITIONS, :]
        s = lax.dot_general(q, keys, NT, preferred_element_type=jnp.float32) * scale
        s = jnp.where(lane < used_ref[p], s, NEG)
        top = jnp.max(s, axis=1, keepdims=True)
        w = jnp.exp(s - top).astype(jnp.bfloat16)
        total_w = jnp.sum(w.astype(jnp.float32), axis=1, keepdims=True)
        o_buf[pl.ds(pl.multiple_of(p * GROUP, GROUP), GROUP), :] = jnp.dot(
            w, values, preferred_element_type=jnp.float32
        )
        mine = lane == lane0 + j
        tops = jnp.where(mine, top, tops)
        sums = jnp.where(mine, total_w, sums)
    top_buf[chunk] = tops
    sum_buf[chunk] = sums

    @pl.when(step == pl.num_programs(0) - 1)
    def _():
        chunks = pages // 128
        top = jnp.concatenate([top_buf[c] for c in range(chunks)], axis=1)
        page_sum = jnp.concatenate([sum_buf[c] for c in range(chunks)], axis=1)
        at = jnp.broadcast_to(row_ref[...], (GROUP, pages))
        where = lax.broadcasted_iota(jnp.int32, (GROUP, pages), 1)
        ahead, behind = segment_scan(top, at, where, pages, jnp.maximum, NEG)
        slot_top = jnp.maximum(ahead, behind)
        factor = jnp.exp(top - slot_top)
        part = page_sum * factor
        ahead, behind = segment_scan(part, at, where, pages, jnp.add, 0.0)
        slot_sum = ahead + behind - part
        slot_sum = jnp.maximum(slot_sum, part)
        lse = slot_top + jnp.log(slot_sum)
        first = first_ref[...].astype(jnp.float32)
        high = lse.astype(jnp.bfloat16).astype(jnp.float32)
        rest = lse - high
        middle = rest.astype(jnp.bfloat16).astype(jnp.float32)
        low = rest - middle
        stacked = jnp.concatenate(
            [
                high * first,
                middle * first,
                low * first,
                factor / slot_sum,
                jnp.zeros((STATS - 4 * GROUP, pages), jnp.float32),
            ],
            axis=0,
        )
        turned = stacked.T
        hot = row_ref[...] == lax.broadcasted_iota(jnp.int32, (total, pages), 0)
        hot = jnp.where(hot, 1.0, 0.0).astype(jnp.bfloat16)
        for h in range(GROUP):
            values = o_buf[pl.ds(h, pages, stride=GROUP), :]
            at_h = 3 * GROUP + h
            values = (values * turned[:, at_h : at_h + 1]).astype(jnp.bfloat16)
            out_ref[:, h * HEAD_WIDTH : (h + 1) * HEAD_WIDTH] = jnp.dot(
                hot, values, preferred_element_type=jnp.float32
            ).astype(jnp.bfloat16)
        column = lax.broadcasted_iota(jnp.int32, (pages, STATS), 1)
        stats = jnp.where(column < 3 * GROUP, turned, 0.0).astype(jnp.bfloat16)
        out_ref[:, GROUP * HEAD_WIDTH :] = jnp.dot(
            hot, stats, preferred_element_type=jnp.float32
        ).astype(jnp.bfloat16)


def finish_kernel(
    n, kv, entries, row_ref, query_ref, latest_ref, slots_ref, weight_ref, out_ref,
    got, weight, attended, partial, parts, send_sem, recv_sem, kv_send, kv_recv, own_sem, w_sem,
):
    me = lax.axis_index("req")
    me_kv = lax.axis_index("kv")
    barrier = greet("req", n)
    greet("kv", kv)
    load = pltpu.make_async_copy(weight_ref, weight, w_sem)
    own = pltpu.make_async_copy(slots_ref.at[me], got.at[me], own_sem)
    own.start()
    pl.semaphore_wait(barrier, n + kv - 2)
    copies = []
    for step in range(1, n):
        peer = lax.rem(me + step, n)
        copy = pltpu.make_async_remote_copy(
            src_ref=slots_ref.at[peer],
            dst_ref=got.at[me],
            send_sem=send_sem.at[step],
            recv_sem=recv_sem.at[step],
            device_id={"req": peer},
            device_id_type=MESH,
        )
        copy.start()
        copies.append(copy)
    load.start()
    rows = query_ref.shape[0]
    total = n * entries
    scale = HEAD_WIDTH ** (-0.5)
    latest_key = latest_ref[0].astype(jnp.float32)
    latest_value = latest_ref[1].astype(jnp.float32)
    mine = row_ref[...] == lax.broadcasted_iota(jnp.int32, (rows, total), 0)
    selfs = []
    for h in range(GROUP):
        q = query_ref[:, h * HEAD_WIDTH : (h + 1) * HEAD_WIDTH].astype(jnp.float32)
        selfs.append(jnp.sum(q * latest_key, axis=1, keepdims=True) * scale)
    own.wait()
    for copy in copies:
        copy.wait()
    width = GROUP * HEAD_WIDTH
    head = lax.broadcasted_iota(jnp.int32, (GROUP, STATS), 0)
    column = lax.broadcasted_iota(jnp.int32, (GROUP, STATS), 1)
    chosen = (column == head) | (column == head + GROUP) | (column == head + 2 * GROUP)
    chosen = jnp.where(chosen, 1.0, 0.0).astype(jnp.bfloat16)
    lse = lax.dot_general(
        chosen,
        got[:, :, width:].reshape(total, STATS),
        NT,
        preferred_element_type=jnp.float32,
    )
    for h in range(GROUP):
        score = jnp.where(mine, lse[h : h + 1, :], NEG)
        top = jnp.maximum(jnp.max(score, axis=1, keepdims=True), selfs[h])
        w = jnp.exp(score - top)
        own_factor = jnp.exp(selfs[h] - top)
        denominator = jnp.sum(w, axis=1, keepdims=True) + own_factor
        w_high = w.astype(jnp.bfloat16)
        w_low = (w - w_high.astype(jnp.float32)).astype(jnp.bfloat16)
        values = got[:, :, h * HEAD_WIDTH : (h + 1) * HEAD_WIDTH].reshape(total, HEAD_WIDTH)
        numerator = (
            jnp.dot(w_high, values, preferred_element_type=jnp.float32)
            + jnp.dot(w_low, values, preferred_element_type=jnp.float32)
            + latest_value * own_factor
        )
        attended[:, h * HEAD_WIDTH : (h + 1) * HEAD_WIDTH] = (numerator / denominator).astype(
            jnp.bfloat16
        )
    load.wait()
    block = weight.shape[1] // kv

    def project(target):
        return jnp.dot(
            attended[...],
            weight[:, pl.ds(pl.multiple_of(target * block, block), block)],
            preferred_element_type=jnp.float32,
        )

    copies = []
    for step in range(1, kv):
        peer = lax.rem(me_kv + step, kv)
        partial[step] = project(peer).astype(jnp.bfloat16)
        copy = pltpu.make_async_remote_copy(
            src_ref=partial.at[step],
            dst_ref=parts.at[step],
            send_sem=kv_send.at[step],
            recv_sem=kv_recv.at[step],
            device_id={"kv": peer},
            device_id_type=MESH,
        )
        copy.start()
        copies.append(copy)
    result = project(me_kv)
    for step, copy in enumerate(copies, 1):
        copy.wait()
        result = result + parts[step].astype(jnp.float32)
    out_ref[...] = result.astype(jnp.bfloat16)


def per_device(query, latest_key_value, cache, out_weight, home, pieces, lengths):
    n = lax.axis_size("req")
    kv = lax.axis_size("kv")
    me = lax.axis_index("req")
    rows, width = query.shape
    extra = pieces.shape[1] // n
    page_count = cache.shape[1] // PAGE_POSITIONS
    entries, row_of_entry, page_at, page_used, page_first = tables(
        home, pieces, lengths, me, n, rows, extra, page_count
    )
    total = n * entries
    bf16, f32 = jnp.bfloat16, jnp.float32
    vmem = pl.BlockSpec(memory_space=pltpu.VMEM)
    anywhere = pl.BlockSpec(memory_space=pl.ANY)
    dma = pltpu.SemaphoreType.DMA
    arrived = pl.pallas_call(
        functools.partial(send_kernel, n, entries),
        name="send_queries",
        out_shape=jax.ShapeDtypeStruct((n, entries, width), bf16),
        in_specs=[vmem, vmem],
        out_specs=anywhere,
        scratch_shapes=[pltpu.VMEM((n, entries, width), bf16), dma((n,)), dma((n,)), dma],
        compiler_params=pltpu.CompilerParams(collective_id=0, has_side_effects=True),
    )(row_of_entry.reshape(total, 1), query)

    block = PAGE_BLOCK * PAGE_POSITIONS
    whole = lambda shape: pl.BlockSpec(shape, lambda i, used: (0,) * len(shape))
    slots = pl.pallas_call(
        attention_kernel,
        name="attend_pages",
        out_shape=jax.ShapeDtypeStruct((total, width + STATS), bf16),
        grid_spec=pltpu.PrefetchScalarGridSpec(
            num_scalar_prefetch=1,
            grid=(page_count // PAGE_BLOCK,),
            in_specs=[
                whole((page_count, 1)),
                whole((1, page_count)),
                whole((1, page_count)),
                whole((total, width)),
                pl.BlockSpec((1, block, HEAD_WIDTH), lambda i, used: (0, i, 0)),
                pl.BlockSpec((1, block, HEAD_WIDTH), lambda i, used: (1, i, 0)),
            ],
            out_specs=whole((total, width + STATS)),
            scratch_shapes=[
                pltpu.VMEM((page_count * GROUP, HEAD_WIDTH), f32),
                pltpu.VMEM((page_count * GROUP, HEAD_WIDTH), f32),
                pltpu.VMEM((page_count // 128, GROUP, 128), f32),
                pltpu.VMEM((page_count // 128, GROUP, 128), f32),
            ],
        ),
        compiler_params=pltpu.CompilerParams(vmem_limit_bytes=40 << 20),
    )(
        page_used,
        page_at.reshape(page_count, 1),
        page_at.reshape(1, page_count),
        page_first.reshape(1, page_count),
        arrived.reshape(total, width),
        cache,
        cache,
    )

    out_width = out_weight.shape[1] // kv
    return pl.pallas_call(
        functools.partial(finish_kernel, n, kv, entries),
        name="combine_project",
        out_shape=jax.ShapeDtypeStruct((rows, out_width), bf16),
        in_specs=[vmem, vmem, vmem, anywhere, anywhere],
        out_specs=vmem,
        scratch_shapes=[
            pltpu.VMEM((n, entries, width + STATS), bf16),
            pltpu.VMEM(out_weight.shape, bf16),
            pltpu.VMEM((rows, width), bf16),
            pltpu.VMEM((kv, rows, out_width), bf16),
            pltpu.VMEM((kv, rows, out_width), bf16),
            dma((n,)),
            dma((n,)),
            dma((kv,)),
            dma((kv,)),
            dma,
            dma,
        ],
        compiler_params=pltpu.CompilerParams(
            collective_id=1, has_side_effects=True, vmem_limit_bytes=40 << 20
        ),
    )(
        row_of_entry.reshape(1, total),
        query,
        latest_key_value,
        slots.reshape(n, entries, width + STATS),
        out_weight,
    )


def solution(mesh):
    placed = (
        P("req", "kv"),
        P(None, "req", "kv"),
        P(None, "req", "kv"),
        P("kv", None),
        P(),
        P(),
        P(),
    )
    return jax.shard_map(
        per_device, mesh=mesh, in_specs=placed, out_specs=P("req", "kv"), check_vma=False
    )
```

time: 183 us -> 157 us (0.86)
  the two profiles are of different devices: /device:TPU:0 before, /device:TPU:9 now
where the time goes in v1:
time: 157 us; the launch traced here: 156 us
  Pallas kernels  143 us (91%)
  local copies, waits for them, and re-layouts  6.63 us (4%)
  other arithmetic  6.32 us (4%)
    pallas_call x1, Pallas kernels, per_device(): pl.pallas_call(attention_kernel, name='attend_pages', out_shape=jax.Shape...  95.3 us
    pallas_call x1, Pallas kernels, per_device(): pl.pallas_call(functools.partial(finish_kernel, n, kv, entries), name='co...  33.9 us
    pallas_call x1, Pallas kernels, per_device(): pl.pallas_call(functools.partial(send_kernel, n, entries), name='send_que...  13.7 us
    unnamed x9, local copies, waits for them, and re-layouts  5.19 us

profile of v1, /device:TPU:9, one launch (start us, length us, event | category | flops | bytes accessed | tf_op | source)
XLA Modules:
  0.0 156.1 jit_solution(16727029785056604747)
XLA Ops:
  0.0 0.7 and_reduce_fusion
  0.7 0.1 and.81
  0.8 0.7 add_select_fusion.2
  1.5 0.1 eq.42
  1.6 0.8 slice_reduce_fusion.1
  2.4 0.3 select_reduce_fusion
  2.7 0.7 sub.82
  3.4 0.1 dynamic-slice_bitcast_fusion
  3.5 0.1 div.55
  3.6 0.6 convert_reduce_fusion.1
  4.2 0.1 reshape.187
  4.3 0.1 add.113
  4.3 0.7 multiply_add_fusion
  5.0 0.9 fusion.1
  5.9 0.1 dynamic_slice.7
  6.0 0.1 pad_add_fusion.2
  6.1 0.1 pad_add_fusion.1
  6.2 0.1 select_reduce_fusion.4
  6.3 0.2 convert_reduce_fusion.2
  6.6 0.3 select_reduce_fusion.1
  6.9 0.8 sub.90.row_ref
  7.7 0.1 reshape.193.col_ref
  7.8 13.7 %send_queries.1 = bf16[8,48,1024]{2,1,0:T(8,128)(2,1)} custom-call(s32[384,1]{1,0:T(8,128)} %sub.90.row_ref, bf16[96,1024]{1,0:T(8,128)(2,1)} %query_ref.3), custom_call_target="tpu_custom_call" | custom-call | tf_op jit(solution)/shard_map/send_queries/pallas_call | solution.py:333
  21.6 0.0 copy-start.1
  21.6 1.1 copy-done.1
  22.7 0.0 copy-start.2
  22.7 0.0 copy-start.3
  22.7 95.3 %attend_pages.1 = bf16[384,1152]{1,0:T(8,128)(2,1)S(1)} custom-call(s32[384]{0:T(512)S(1)} %get-tuple-element.14.used_ref, s32[384,1]{1,0:T(8,128)S(1)} %reshape.193.col_ref, s32[1,384]{1,0:T(1,128)S(1)} %reshape.189.row_ref, s32[1,384]{1,0:T(1,128)S(1)} %reshape.190.first_ref, bf16[384,1024]{1,0:T(8,128)(2,1)S(1)} %bitcast.5, ...), custom_call_target="tpu_custom_call" | custom-call | tf_op jit(solution)/shard_map/attend_pages/pallas_call | solution.py:345
  118.1 0.0 copy-done.2
  118.1 0.0 copy-done.3
  118.1 0.0 copy-start
  118.1 3.4 %copy-done = bf16[1024,4096]{1,0:T(8,128)(2,1)S(1)} copy-done((bf16[1024,4096]{1,0:T(8,128)(2,1)S(1)}, bf16[1024,4096]{1,0:T(8,128)(2,1)}, u32[]{:S(2)}) %copy-start) | copy-done | bytes 8388632
  121.5 33.9 %combine_project.1 = bf16[96,1024]{1,0:T(8,128)(2,1)S(1)} custom-call(s32[1,384]{1,0:T(1,128)S(1)} %sub.81.row_ref, bf16[96,1024]{1,0:T(8,128)(2,1)S(1)} %copy-done.2, bf16[2,96,128]{2,1,0:T(8,128)(2,1)S(1)} %copy-done.3, bf16[8,48,1152]{2,1,0:T(8,128)(2,1)S(1)} %bitcast.4, bf16[1024,4096]{1,0:T(8,128)(2,1)S(1)} %copy-done), custom_call_target="tpu_custom_call" | custom-call | tf_op jit(solution)/shard_map/combine_project/pallas_call | solution.py:380
  155.4 0.7 copy.13
  (12 shorter events, 0.1 us)
Async XLA Ops:
  21.6 1.1 copy-start.1
  22.7 95.4 %copy-start.2 = (bf16[96,1024]{1,0:T(8,128)(2,1)S(1)}, bf16[96,1024]{1,0:T(8,128)(2,1)}, u32[]{:S(2)}) copy-start(bf16[96,1024]{1,0:T(8,128)(2,1)} %query_ref.3) | copy-start | bytes 589828
  22.7 95.4 %copy-start.3 = (bf16[2,96,128]{2,1,0:T(8,128)(2,1)S(1)}, bf16[2,96,128]{2,1,0:T(8,128)(2,1)}, u32[]{:S(2)}) copy-start(bf16[2,96,128]{2,1,0:T(8,128)(2,1)} %latest_ref.1) | copy-start | bytes 147460
  118.1 3.4 %copy-start = (bf16[1024,4096]{1,0:T(8,128)(2,1)S(1)}, bf16[1024,4096]{1,0:T(8,128)(2,1)}, u32[]{:S(2)}) copy-start(bf16[1024,4096]{1,0:T(8,128)(2,1)} %weight_ref.1) | copy-start | bytes 25165828

commit v2 on v1

--- a/solution.py
+++ b/solution.py
@@ -146,27 +146,42 @@
             )
 
     lane = lax.broadcasted_iota(jnp.int32, (GROUP, 128), 1)
+    pair = (2 * GROUP, 2 * PAGE_POSITIONS)
+    column = lax.broadcasted_iota(jnp.int32, pair, 1)
+    upper = lax.broadcasted_iota(jnp.int32, pair, 0) < GROUP
+    column = jnp.where(upper, column, column - PAGE_POSITIONS)
+    column = jnp.where(column < 0, 2 * PAGE_POSITIONS, column)
     per_chunk = 128 // PAGE_BLOCK
     lane0 = lax.rem(step, per_chunk) * PAGE_BLOCK
     chunk = step // per_chunk
     tops = top_buf[chunk]
     sums = sum_buf[chunk]
-    for j in range(PAGE_BLOCK):
-        p = step * PAGE_BLOCK + j
-        q = q_buf[pl.ds(pl.multiple_of(p * GROUP, GROUP), GROUP), :].astype(jnp.bfloat16)
-        keys = key_ref[0, j * PAGE_POSITIONS : (j + 1) * PAGE_POSITIONS, :]
-        values = value_ref[0, j * PAGE_POSITIONS : (j + 1) * PAGE_POSITIONS, :]
-        s = lax.dot_general(q, keys, NT, preferred_element_type=jnp.float32) * scale
-        s = jnp.where(lane < used_ref[p], s, NEG)
+    row0 = pl.multiple_of(step * (PAGE_BLOCK * GROUP), PAGE_BLOCK * GROUP)
+    batch = PAGE_BLOCK // 2
+    scores = []
+    for j in range(batch):
+        q = q_buf[pl.ds(row0 + j * 2 * GROUP, 2 * GROUP), :].astype(jnp.bfloat16)
+        keys = key_ref[0, j * 2 * PAGE_POSITIONS : (j + 1) * 2 * PAGE_POSITIONS, :]
+        scores.append(lax.dot_general(q, keys, NT, preferred_element_type=jnp.float32))
+    weights = []
+    for j in range(batch):
+        p = step * PAGE_BLOCK + 2 * j
+        in_use = column < jnp.where(upper, used_ref[p], used_ref[p + 1])
+        s = jnp.where(in_use, scores[j] * scale, NEG)
         top = jnp.max(s, axis=1, keepdims=True)
         w = jnp.exp(s - top).astype(jnp.bfloat16)
         total_w = jnp.sum(w.astype(jnp.float32), axis=1, keepdims=True)
-        o_buf[pl.ds(pl.multiple_of(p * GROUP, GROUP), GROUP), :] = jnp.dot(
-            w, values, preferred_element_type=jnp.float32
-        )
-        mine = lane == lane0 + j
-        tops = jnp.where(mine, top, tops)
-        sums = jnp.where(mine, total_w, sums)
+        weights.append(w)
+        for k in range(2):
+            mine = lane == lane0 + 2 * j + k
+            tops = jnp.where(mine, top[k * GROUP : (k + 1) * GROUP], tops)
+            sums = jnp.where(mine, total_w[k * GROUP : (k + 1) * GROUP], sums)
+    results = []
+    for j in range(batch):
+        values = value_ref[0, j * 2 * PAGE_POSITIONS : (j + 1) * 2 * PAGE_POSITIONS, :]
+        results.append(jnp.dot(weights[j], values, preferred_element_type=jnp.float32))
+    for j in range(batch):
+        o_buf[pl.ds(row0 + j * 2 * GROUP, 2 * GROUP), :] = results[j]
     top_buf[chunk] = tops
     sum_buf[chunk] = sums
 
@@ -365,7 +380,7 @@
                 pltpu.VMEM((page_count // 128, GROUP, 128), f32),
             ],
         ),
-        compiler_params=pltpu.CompilerParams(vmem_limit_bytes=40 << 20),
+        compiler_params=pltpu.CompilerParams(vmem_limit_bytes=56 << 20),
     )(
         page_used,
         page_at.reshape(page_count, 1),
@@ -397,7 +412,7 @@
             dma,
         ],
         compiler_params=pltpu.CompilerParams(
-            collective_id=1, has_side_effects=True, vmem_limit_bytes=40 << 20
+            collective_id=1, has_side_effects=True, vmem_limit_bytes=56 << 20
         ),
     )(
         row_of_entry.reshape(1, total),

time: 157 us -> 81.4 us (0.52)
  Pallas kernels: 143 us -> 68.4 us
    pallas_call x1, Pallas kernels: 95.3 us -> 18.8 us  [per_device(): pl.pallas_call(attention_kernel, name='attend_pages', out_shape=jax.Shape...]
    unnamed x9 -> x1, local copies, waits for them, and re-layouts: 5.19 us -> 1.62 us
    pallas_call x1, Pallas kernels: 33.9 us -> 35.9 us  [per_device(): pl.pallas_call(functools.partial(finish_kernel, n, kv, entries), name='co...]
where the time goes in v2:
time: 81.4 us; the launch traced here: 80.9 us
  Pallas kernels  68.4 us (84%)
  other arithmetic  6.92 us (9%)
  local copies, waits for them, and re-layouts  5.47 us (7%)
    pallas_call x1, Pallas kernels, per_device(): pl.pallas_call(functools.partial(finish_kernel, n, kv, entries), name='co...  35.9 us
    pallas_call x1, Pallas kernels, per_device(): pl.pallas_call(attention_kernel, name='attend_pages', out_shape=jax.Shape...  18.8 us
    pallas_call x1, Pallas kernels, per_device(): pl.pallas_call(functools.partial(send_kernel, n, entries), name='send_que...  13.7 us

profile of v2, /device:TPU:9, one launch (start us, length us, event | category | flops | bytes accessed | tf_op | source)
XLA Modules:
  0.0 80.9 jit_solution(14668199687676356943)
XLA Ops:
  0.0 0.7 and_reduce_fusion
  0.7 0.1 and.81
  0.8 0.7 add_select_fusion.2
  1.5 0.1 eq.42
  1.6 0.8 slice_reduce_fusion.1
  2.4 0.3 select_reduce_fusion
  2.7 0.7 sub.82
  3.4 0.1 dynamic-slice_bitcast_fusion
  3.5 0.1 div.55
  3.6 0.6 convert_reduce_fusion.1
  4.2 0.1 reshape.187
  4.3 0.1 add.113
  4.3 0.7 multiply_add_fusion
  5.0 0.9 %fusion.1 = (s32[96]{0:T(128)S(1)}, s32[96]{0:T(128)S(1)}) fusion(s32[768]{0:T(1024)S(1)} %get-tuple-element.23, s32[768]{0:T(1024)} %param.11, s32[96]{0:T(128)S(1)} %iota_add_fusion, s32[768]{0:T(1024)S(1)} %sub.82), kind=kLoop, calls=%fused_computation.9 | loop fusion | flops 368448 | bytes 10368 | tf_op jit(solution)/shard_map/reduce_sum | solution.py:53
  5.9 0.1 dynamic_slice.7
  6.0 0.1 pad_add_fusion.2
  6.1 0.1 pad_add_fusion.1
  6.2 0.1 select_reduce_fusion.4
  6.3 0.8 %convert_reduce_fusion.2 = (s32[384]{0:T(512)S(1)}, s32[384]{0:T(512)S(1)}, s32[384]{0:T(512)}) fusion(s32[192]{0:T(256)S(1)} %add.120, s32[192]{0:T(256)S(1)} %select_reduce_fusion.4, s32[192]{0:T(256)S(1)} %pad_add_fusion.2, s32[192]{0:T(256)S(1)} %get-tuple-element.20), kind=kLoop, calls=%fused_computation.10 | loop fusion | flops 1104768 | bytes 7680 | tf_op jit(solution)/shard_map/reduce_sum | solution.py:70
  7.2 0.6 reshape.190.first_ref
  7.7 0.6 reshape.189.row_ref
  8.3 0.3 select_reduce_fusion.1
  8.7 0.6 sub.81.row_ref
  9.2 0.8 sub.90.row_ref
  10.0 0.8 reshape.193.col_ref
  10.8 13.7 %send_queries.1 = bf16[8,48,1024]{2,1,0:T(8,128)(2,1)} custom-call(s32[384,1]{1,0:T(8,128)} %sub.90.row_ref, bf16[96,1024]{1,0:T(8,128)(2,1)} %query_ref.3), custom_call_target="tpu_custom_call" | custom-call | tf_op jit(solution)/shard_map/send_queries/pallas_call | solution.py:348
  24.6 18.8 %attend_pages.1 = bf16[384,1152]{1,0:T(8,128)(2,1)} custom-call(s32[384]{0:T(512)} %get-tuple-element.14.used_ref, s32[384,1]{1,0:T(8,128)} %reshape.193.col_ref, s32[1,384]{1,0:T(1,128)} %reshape.189.row_ref, s32[1,384]{1,0:T(1,128)} %reshape.190.first_ref, bf16[384,1024]{1,0:T(8,128)(2,1)} %bitcast.5, bf16[2,49152,128]{2,1,0:T(8,128)(2,1)} %value_ref.1, ...), custom_call_target="tpu_custom_call" | custom-call | tf_op jit(solution)/shard_map/attend_pages/pallas_call | solution.py:360
  43.4 35.9 %combine_project.1 = bf16[96,1024]{1,0:T(8,128)(2,1)} custom-call(s32[1,384]{1,0:T(1,128)} %sub.81.row_ref, bf16[96,1024]{1,0:T(8,128)(2,1)} %query_ref.3, bf16[2,96,128]{2,1,0:T(8,128)(2,1)} %latest_ref.1, bf16[8,48,1152]{2,1,0:T(8,128)(2,1)} %bitcast.4, bf16[1024,4096]{1,0:T(8,128)(2,1)} %weight_ref.1), custom_call_target="tpu_custom_call" | custom-call | tf_op jit(solution)/shard_map/combine_project/pallas_call | solution.py:395
  79.3 1.6 %copy.13 = bf16[96,1024]{1,0:T(8,128)(2,1)} copy(bf16[96,1024]{1,0:T(8,128)(2,1)} %combine_project.1) | data formatting | bytes 393216
  (9 shorter events, 0.1 us)

commit v3 on v2

--- a/solution.py
+++ b/solution.py
@@ -51,12 +51,16 @@
     my_slots = me * rows + jnp.arange(rows, dtype=i32)
     hot = home[None, :] == my_slots[:, None]
     at_home = jnp.sum(jnp.where(hot, (request // rows * entries + home_rank)[None, :], 0), axis=1)
+    home_request = jnp.sum(jnp.where(hot, request[None, :], 0), axis=1)
     moved = jnp.sum(
         jnp.where(request[:, None] == piece_req[None, :], piece_len[None, :], 0), axis=1
     )
     home_len = jnp.sum(jnp.where(hot, (lengths - moved)[None, :], 0), axis=1)
     guest_at = lax.dynamic_slice_in_dim(piece_src * entries + piece_rank, me * extra, extra)
     guest_len = lax.dynamic_slice_in_dim(piece_len, me * extra, extra)
+    guest_request = lax.dynamic_slice_in_dim(piece_req, me * extra, extra)
+    slot_request = jnp.concatenate([home_request, guest_request])
+    slot_row = jnp.bitwise_xor(slot_request // rows, me) * rows + slot_request % rows
     slot_at = jnp.concatenate([at_home, guest_at])
     slot_len = jnp.concatenate([home_len, guest_len])
     per_slot = (slot_len + PAGE_POSITIONS - 1) // PAGE_POSITIONS
@@ -65,10 +69,11 @@
     page = jnp.arange(page_count, dtype=i32)[:, None]
     held = (begin[None, :] <= page) & (page < (begin + per_slot)[None, :])
     page_at = jnp.sum(jnp.where(held, slot_at[None, :], 0), axis=1)
+    page_row = jnp.sum(jnp.where(held, slot_row[None, :], 0), axis=1)
     left = slot_len[None, :] - (page - begin[None, :]) * PAGE_POSITIONS
     page_used = jnp.sum(jnp.where(held, jnp.clip(left, 0, PAGE_POSITIONS), 0), axis=1)
     page_first = jnp.sum((held & (page == begin[None, :])).astype(i32), axis=1)
-    return entries, row_of_entry, page_at, page_used, page_first
+    return entries, row_of_entry, page_at, page_row, page_used, page_first
 
 
 def greet(axis, n):
@@ -80,37 +85,13 @@
     return barrier
 
 
-def send_kernel(n, entries, row_ref, query_ref, out_ref, packed, send_sem, recv_sem, own_sem):
-    me = lax.axis_index("req")
-    barrier = greet("req", n)
-    rows = query_ref.shape[0]
-    pick = row_ref[...] == lax.broadcasted_iota(jnp.int32, (n * entries, rows), 1)
-    pick = jnp.where(pick, 1.0, 0.0).astype(jnp.bfloat16)
-    width = query_ref.shape[1]
-    packed[...] = (
-        jnp.dot(pick, query_ref[...], preferred_element_type=jnp.float32)
-        .astype(jnp.bfloat16)
-        .reshape(n, entries, width)
-    )
-    own = pltpu.make_async_copy(packed.at[me], out_ref.at[me], own_sem)
-    own.start()
-    pl.semaphore_wait(barrier, n - 1)
-    copies = []
-    for step in range(1, n):
-        peer = lax.rem(me + step, n)
-        copy = pltpu.make_async_remote_copy(
-            src_ref=packed.at[peer],
-            dst_ref=out_ref.at[me],
-            send_sem=send_sem.at[step],
-            recv_sem=recv_sem.at[step],
-            device_id={"req": peer},
-            device_id_type=MESH,
-        )
-        copy.start()
-        copies.append(copy)
-    own.wait()
-    for copy in copies:
-        copy.wait()
+def spread_queries(query, n):
+    def swap(block, k):
+        return lax.ppermute(block, "req", [(i, i ^ k) for i in range(n)])
+
+    blocks = [query] + [swap(query, k) for k in range(2, n, 2)]
+    handed = [swap(block, 1) for block in blocks]
+    return [block for both in zip(blocks, handed) for block in both]
 
 
 def segment_scan(x, at, lane, width, combine, empty):
@@ -126,22 +107,25 @@
 
 
 def attention_kernel(
-    used_ref, col_ref, row_ref, first_ref, arrived_ref, key_ref, value_ref,
-    out_ref, q_buf, o_buf, top_buf, sum_buf,
+    used_ref, col_ref, row_ref, first_ref, *refs
 ):
+    (*block_refs, key_ref, value_ref, out_ref, q_all, q_buf, o_buf, top_buf, sum_buf) = refs
     step = pl.program_id(0)
     pages = col_ref.shape[0]
-    total = arrived_ref.shape[0]
+    total = out_ref.shape[0]
+    requests, rows = q_all.shape[0], block_refs[0].shape[0]
     scale = HEAD_WIDTH ** (-0.5)
 
     @pl.when(step == 0)
     def _():
-        hot = col_ref[...] == lax.broadcasted_iota(jnp.int32, (pages, total), 1)
+        for k, block_ref in enumerate(block_refs):
+            q_all[k * rows : (k + 1) * rows, :] = block_ref[...]
+        hot = col_ref[...] == lax.broadcasted_iota(jnp.int32, (pages, requests), 1)
         hot = jnp.where(hot, 1.0, 0.0).astype(jnp.bfloat16)
         for h in range(GROUP):
             q_buf[pl.ds(h, pages, stride=GROUP), :] = jnp.dot(
                 hot,
-                arrived_ref[:, h * HEAD_WIDTH : (h + 1) * HEAD_WIDTH],
+                q_all[:, h * HEAD_WIDTH : (h + 1) * HEAD_WIDTH],
                 preferred_element_type=jnp.float32,
             )
 
@@ -170,12 +154,16 @@
         s = jnp.where(in_use, scores[j] * scale, NEG)
         top = jnp.max(s, axis=1, keepdims=True)
         w = jnp.exp(s - top).astype(jnp.bfloat16)
-        total_w = jnp.sum(w.astype(jnp.float32), axis=1, keepdims=True)
         weights.append(w)
         for k in range(2):
             mine = lane == lane0 + 2 * j + k
             tops = jnp.where(mine, top[k * GROUP : (k + 1) * GROUP], tops)
-            sums = jnp.where(mine, total_w[k * GROUP : (k + 1) * GROUP], sums)
+    ones = jnp.ones((2 * PAGE_POSITIONS, 128), jnp.bfloat16)
+    totals = jnp.dot(
+        jnp.concatenate(weights, axis=0), ones, preferred_element_type=jnp.float32
+    )
+    for p in range(PAGE_BLOCK):
+        sums = jnp.where(lane == lane0 + p, totals[p * GROUP : (p + 1) * GROUP], sums)
     results = []
     for j in range(batch):
         values = value_ref[0, j * 2 * PAGE_POSITIONS : (j + 1) * 2 * PAGE_POSITIONS, :]
@@ -337,7 +325,7 @@
     rows, width = query.shape
     extra = pieces.shape[1] // n
     page_count = cache.shape[1] // PAGE_POSITIONS
-    entries, row_of_entry, page_at, page_used, page_first = tables(
+    entries, row_of_entry, page_at, page_row, page_used, page_first = tables(
         home, pieces, lengths, me, n, rows, extra, page_count
     )
     total = n * entries
@@ -345,16 +333,7 @@
     vmem = pl.BlockSpec(memory_space=pltpu.VMEM)
     anywhere = pl.BlockSpec(memory_space=pl.ANY)
     dma = pltpu.SemaphoreType.DMA
-    arrived = pl.pallas_call(
-        functools.partial(send_kernel, n, entries),
-        name="send_queries",
-        out_shape=jax.ShapeDtypeStruct((n, entries, width), bf16),
-        in_specs=[vmem, vmem],
-        out_specs=anywhere,
-        scratch_shapes=[pltpu.VMEM((n, entries, width), bf16), dma((n,)), dma((n,)), dma],
-        compiler_params=pltpu.CompilerParams(collective_id=0, has_side_effects=True),
-    )(row_of_entry.reshape(total, 1), query)
-
+    blocks = spread_queries(query, n)
     block = PAGE_BLOCK * PAGE_POSITIONS
     whole = lambda shape: pl.BlockSpec(shape, lambda i, used: (0,) * len(shape))
     slots = pl.pallas_call(
@@ -368,12 +347,13 @@
                 whole((page_count, 1)),
                 whole((1, page_count)),
                 whole((1, page_count)),
-                whole((total, width)),
+                *[whole((rows, width))] * n,
                 pl.BlockSpec((1, block, HEAD_WIDTH), lambda i, used: (0, i, 0)),
                 pl.BlockSpec((1, block, HEAD_WIDTH), lambda i, used: (1, i, 0)),
             ],
             out_specs=whole((total, width + STATS)),
             scratch_shapes=[
+                pltpu.VMEM((n * rows, width), bf16),
                 pltpu.VMEM((page_count * GROUP, HEAD_WIDTH), f32),
                 pltpu.VMEM((page_count * GROUP, HEAD_WIDTH), f32),
                 pltpu.VMEM((page_count // 128, GROUP, 128), f32),
@@ -383,10 +363,10 @@
         compiler_params=pltpu.CompilerParams(vmem_limit_bytes=56 << 20),
     )(
         page_used,
-        page_at.reshape(page_count, 1),
+        page_row.reshape(page_count, 1),
         page_at.reshape(1, page_count),
         page_first.reshape(1, page_count),
-        arrived.reshape(total, width),
+        *blocks,
         cache,
         cache,
     )

time: 81.4 us -> 74.9 us (0.920)
  Pallas kernels: 68.4 us -> 56.7 us
  starting transfers between devices: 0 us -> 4.81 us
    pallas_call x1 -> x0, Pallas kernels: 13.7 us -> none  [per_device(): pl.pallas_call(functools.partial(send_kernel, n, entries), name='send_que...]
    ppermute x0 -> x7, starting transfers between devices: none -> 4.81 us  [swap(): return lax.ppermute(block, 'req', [(i, i ^ k) for i in range(n)])]
    pallas_call x1, Pallas kernels: 18.8 us -> 20.3 us  [per_device(): pl.pallas_call(attention_kernel, name='attend_pages', out_shape=jax.Shape...]
    unnamed x1 -> x15, local copies, waits for them, and re-layouts: 1.62 us -> 2.44 us
  transfers between devices with their start and end apart: 0 -> 7, of which waited for: 0 -> 0; matrix products, arithmetic and copies ran while one was open for 0% -> 14% of each run, Pallas kernels for 0% -> 0%
where the time goes in v3:
time: 74.9 us; the launch traced here: 74.3 us
  Pallas kernels  56.7 us (76%)
  other arithmetic  7.09 us (9%)
  local copies, waits for them, and re-layouts  5.53 us (7%)
  starting transfers between devices  4.81 us (6%)
    pallas_call x1, Pallas kernels, per_device(): pl.pallas_call(functools.partial(finish_kernel, n, kv, entries), name='co...  36.4 us
    pallas_call x1, Pallas kernels, per_device(): pl.pallas_call(attention_kernel, name='attend_pages', out_shape=jax.Shape...  20.3 us
    ppermute x7, starting transfers between devices, swap(): return lax.ppermute(block, 'req', [(i, i ^ k) for i in range(n)])  4.81 us
    unnamed x15, local copies, waits for them, and re-layouts  2.44 us
  transfers between devices with their start and end apart: 7, of which 0 were waited for; matrix products, arithmetic and copies ran while one was open for 14% of the time, Pallas kernels for 0%

profile of v3, /device:TPU:9, one launch (start us, length us, event | category | flops | bytes accessed | tf_op | source)
XLA Modules:
  0.0 74.3 jit_solution(5191980267585015816)
XLA Ops:
  0.0 2.2 %collective-permute-start.5 = (bf16[96,1024]{1,0:T(8,128)(2,1)}, bf16[96,1024]{1,0:T(8,128)(2,1)S(1)}, u32[]{:S(2)}, u32[]{:S(2)}) collective-permute-start(bf16[96,1024]{1,0:T(8,128)(2,1)} %query_ref.1), channel_id=1, source_target_pairs={{0,6},{1,7},{2,4},{3,5},{4,2},{5,3},{6,0},{7,1},{8,14},{9,15},{10,... | collective-permute-start | bytes 589832 | tf_op jit(solution)/shard_map/ppermute | solution.py:90
  2.2 0.2 collective-permute-start.3
  2.4 0.3 collective-permute-start.1
  2.7 1.5 %collective-permute-start = (bf16[96,1024]{1,0:T(8,128)(2,1)}, bf16[96,1024]{1,0:T(8,128)(2,1)S(1)}, u32[]{:S(2)}, u32[]{:S(2)}) collective-permute-start(bf16[96,1024]{1,0:T(8,128)(2,1)} %query_ref.1), channel_id=1, source_target_pairs={{0,1},{1,0},{2,3},{3,2},{4,5},{5,4},{6,7},{7,6},{8,9},{9,8},{10,11... | collective-permute-start | bytes 589832 | tf_op jit(solution)/shard_map/ppermute | solution.py:90
  4.2 0.7 and_reduce_fusion
  4.9 0.8 %slice_reduce_fusion = (s32[768]{0:T(1024)S(1)}, s32[768]{0:T(1024)S(1)}, s32[768]{0:T(1024)S(1)}, s32[1,768]{1,0:T(1,128)S(1)}, s32[1,768]{1,0:T(1,128)S(1)}) fusion(s32[2,768]{1,0:T(2,128)} %param.12), kind=kLoop, calls=%fused_computation.64 | loop fusion | flops 768 | bytes 21504 | tf_op jit(solution)/shard_map/slice | solution.py:41
  5.7 0.1 and.96
  5.8 0.7 add_select_fusion.2
  6.5 0.1 eq.44
  6.6 0.3 select_reduce_fusion
  6.9 0.1 div.63
  7.0 0.6 convert_reduce_fusion.1
  7.6 0.1 reshape.226
  7.7 0.1 add.128
  7.8 0.7 sub.84
  8.4 0.7 multiply_add_fusion
  9.2 0.1 dynamic_slice.11
  9.2 0.1 dynamic-slice_bitcast_fusion
  9.3 1.0 %fusion.2 = (s32[96]{0:T(128)S(1)}, s32[96]{0:T(128)S(1)}, s32[96]{0:T(128)S(1)}) fusion(s32[768]{0:T(1024)S(1)} %get-tuple-element.28, s32[768]{0:T(1024)} %param.11, s32[96]{0:T(128)S(1)} %iota_add_fusion, s32[768]{0:T(1024)S(1)} %sub.84), kind=kLoop, calls=%fused_computation.11 | loop fusion | flops 515808 | bytes 10752 | tf_op jit(solution)/shard_map/reduce_sum | solution.py:53
  10.3 0.1 pad_add_fusion.1
  10.3 0.1 select_reduce_fusion.5
  10.5 0.1 fusion.11
  10.6 0.1 pad_add_fusion.3
  10.7 0.9 %convert_reduce_fusion.2 = (s32[384]{0:T(512)S(1)}, s32[384]{0:T(512)S(1)}, s32[384]{0:T(512)}, s32[384]{0:T(512)S(1)}) fusion(s32[192]{0:T(256)S(1)} %select_reduce_fusion.5, s32[192]{0:T(256)S(1)} %add.135, s32[192]{0:T(256)S(1)} %pad_add_fusion.3, s32[192]{0:T(256)S(1)} %get-tuple-element.23, s32[192]{0:T(256)S(1)} %fusion.11), kind=kLoop, calls=%fused_computation.12 | loop fusion | flops 1251840 | bytes 9984 | tf_op jit(solution)/shard_map/reduce_sum | solution.py:75
  11.5 0.6 reshape.229.first_ref
  12.1 0.6 reshape.228.row_ref
  12.7 0.3 select_reduce_fusion.1
  13.0 0.0 collective-permute-done.5.refs_6_
  13.0 0.0 copy-start
  13.0 0.1 collective-permute-start.6
  13.1 0.0 collective-permute-done.3.refs_4_
  13.1 0.0 copy-start.1
  13.1 0.5 collective-permute-start.4
  13.6 0.0 collective-permute-done.1.refs_2_
  13.6 0.0 copy-start.2
  13.6 0.1 collective-permute-start.2
  13.7 0.6 sub.83.row_ref
  14.3 0.8 %reshape.231.col_ref = s32[384,1]{1,0:T(8,128)} reshape(s32[384]{0:T(512)S(1)} %get-tuple-element.16) | data formatting | bytes 3072 | tf_op jit(solution)/shard_map/reshape | solution.py:366
  15.1 0.0 collective-permute-done.refs_1_
  15.1 0.0 copy-start.3
  15.1 0.0 collective-permute-done.6.refs_7_
  15.1 0.0 copy-start.4
  15.1 0.0 collective-permute-done.4.refs_5_
  15.1 0.0 copy-start.5
  15.1 0.0 collective-permute-done.2.refs_3_
  15.2 0.0 copy-start.6
  15.2 0.0 copy-done
  15.2 0.0 copy-done.1
  15.2 0.0 copy-done.2
  15.2 0.6 copy-done.3
  15.8 0.1 copy-done.4
  15.9 0.1 copy-done.5
  15.9 0.1 copy-done.6
  16.0 20.3 %attend_pages.1 = bf16[384,1152]{1,0:T(8,128)(2,1)} custom-call(s32[384]{0:T(512)} %get-tuple-element.15.used_ref, s32[384,1]{1,0:T(8,128)} %reshape.231.col_ref, s32[1,384]{1,0:T(1,128)} %reshape.228.row_ref, s32[1,384]{1,0:T(1,128)} %reshape.229.first_ref, bf16[96,1024]{1,0:T(8,128)(2,1)} %query_ref.1, bf16[96,1024]{1,0:T(8,128)(2,1)} %copy-done.3, ...), custom_call_target="tpu_custom_call" | custom-call | tf_op jit(solution)/shard_map/attend_pages/pallas_call | solution.py:339
  36.3 36.4 %combine_project.1 = bf16[96,1024]{1,0:T(8,128)(2,1)} custom-call(s32[1,384]{1,0:T(1,128)} %sub.83.row_ref, bf16[96,1024]{1,0:T(8,128)(2,1)} %query_ref.1, bf16[2,96,128]{2,1,0:T(8,128)(2,1)} %latest_ref.1, bf16[8,48,1152]{2,1,0:T(8,128)(2,1)} %bitcast.5, bf16[1024,4096]{1,0:T(8,128)(2,1)} %weight_ref.1), custom_call_target="tpu_custom_call" | custom-call | tf_op jit(solution)/shard_map/combine_project/pallas_call | solution.py:375
  72.7 1.6 %copy.11 = bf16[96,1024]{1,0:T(8,128)(2,1)} copy(bf16[96,1024]{1,0:T(8,128)(2,1)} %combine_project.1) | data formatting | bytes 393216
  (9 shorter events, 0.1 us)
Async XLA Ops:
  0.0 13.0 %collective-permute-start.5 = (bf16[96,1024]{1,0:T(8,128)(2,1)}, bf16[96,1024]{1,0:T(8,128)(2,1)S(1)}, u32[]{:S(2)}, u32[]{:S(2)}) collective-permute-start(bf16[96,1024]{1,0:T(8,128)(2,1)} %query_ref.1), channel_id=1, source_target_pairs={{0,6},{1,7},{2,4},{3,5},{4,2},{5,3},{6,0},{7,1},{8,14},{9,15},{10,... | collective-permute-start | bytes 589832 | tf_op jit(solution)/shard_map/ppermute | solution.py:90
  2.2 10.9 %collective-permute-start.3 = (bf16[96,1024]{1,0:T(8,128)(2,1)}, bf16[96,1024]{1,0:T(8,128)(2,1)S(1)}, u32[]{:S(2)}, u32[]{:S(2)}) collective-permute-start(bf16[96,1024]{1,0:T(8,128)(2,1)} %query_ref.1), channel_id=1, source_target_pairs={{0,4},{1,5},{2,6},{3,7},{4,0},{5,1},{6,2},{7,3},{8,12},{9,13},{10,... | collective-permute-start | bytes 589832 | tf_op jit(solution)/shard_map/ppermute | solution.py:90
  2.4 11.2 %collective-permute-start.1 = (bf16[96,1024]{1,0:T(8,128)(2,1)}, bf16[96,1024]{1,0:T(8,128)(2,1)S(1)}, u32[]{:S(2)}, u32[]{:S(2)}) collective-permute-start(bf16[96,1024]{1,0:T(8,128)(2,1)} %query_ref.1), channel_id=1, source_target_pairs={{0,2},{1,3},{2,0},{3,1},{4,6},{5,7},{6,4},{7,5},{8,10},{9,11},{10,... | collective-permute-start | bytes 589832 | tf_op jit(solution)/shard_map/ppermute | solution.py:90
  2.7 12.5 %collective-permute-start = (bf16[96,1024]{1,0:T(8,128)(2,1)}, bf16[96,1024]{1,0:T(8,128)(2,1)S(1)}, u32[]{:S(2)}, u32[]{:S(2)}) collective-permute-start(bf16[96,1024]{1,0:T(8,128)(2,1)} %query_ref.1), channel_id=1, source_target_pairs={{0,1},{1,0},{2,3},{3,2},{4,5},{5,4},{6,7},{7,6},{8,9},{9,8},{10,11... | collective-permute-start | bytes 589832 | tf_op jit(solution)/shard_map/ppermute | solution.py:90
  13.0 2.1 %copy-start = (bf16[96,1024]{1,0:T(8,128)(2,1)}, bf16[96,1024]{1,0:T(8,128)(2,1)S(1)}, u32[]{:S(2)}) copy-start(bf16[96,1024]{1,0:T(8,128)(2,1)S(1)} %collective-permute-done.5.refs_6_) | copy-start | bytes 589828
  13.0 2.1 %collective-permute-start.6 = (bf16[96,1024]{1,0:T(8,128)(2,1)S(1)}, bf16[96,1024]{1,0:T(8,128)(2,1)S(1)}, u32[]{:S(2)}, u32[]{:S(2)}) collective-permute-start(bf16[96,1024]{1,0:T(8,128)(2,1)S(1)} %collective-permute-done.5.refs_6_), channel_id=1, source_target_pairs={{0,1},{1,0},{2,3},{3,2},{4,5},{5,4},{6,7},{7,6},{8,9},{9,8},{10,11... | collective-permute-start | bytes 589832 | tf_op jit(solution)/shard_map/ppermute | solution.py:90
  13.1 2.1 %copy-start.1 = (bf16[96,1024]{1,0:T(8,128)(2,1)}, bf16[96,1024]{1,0:T(8,128)(2,1)S(1)}, u32[]{:S(2)}) copy-start(bf16[96,1024]{1,0:T(8,128)(2,1)S(1)} %collective-permute-done.3.refs_4_) | copy-start | bytes 589828
  13.1 2.0 %collective-permute-start.4 = (bf16[96,1024]{1,0:T(8,128)(2,1)S(1)}, bf16[96,1024]{1,0:T(8,128)(2,1)S(1)}, u32[]{:S(2)}, u32[]{:S(2)}) collective-permute-start(bf16[96,1024]{1,0:T(8,128)(2,1)S(1)} %collective-permute-done.3.refs_4_), channel_id=1, source_target_pairs={{0,1},{1,0},{2,3},{3,2},{4,5},{5,4},{6,7},{7,6},{8,9},{9,8},{10,11... | collective-permute-start | bytes 589832 | tf_op jit(solution)/shard_map/ppermute | solution.py:90
  13.6 1.6 %copy-start.2 = (bf16[96,1024]{1,0:T(8,128)(2,1)}, bf16[96,1024]{1,0:T(8,128)(2,1)S(1)}, u32[]{:S(2)}) copy-start(bf16[96,1024]{1,0:T(8,128)(2,1)S(1)} %collective-permute-done.1.refs_2_) | copy-start | bytes 589828
  13.6 1.5 %collective-permute-start.2 = (bf16[96,1024]{1,0:T(8,128)(2,1)S(1)}, bf16[96,1024]{1,0:T(8,128)(2,1)S(1)}, u32[]{:S(2)}, u32[]{:S(2)}) collective-permute-start(bf16[96,1024]{1,0:T(8,128)(2,1)S(1)} %collective-permute-done.1.refs_2_), channel_id=1, source_target_pairs={{0,1},{1,0},{2,3},{3,2},{4,5},{5,4},{6,7},{7,6},{8,9},{9,8},{10,11... | collective-permute-start | bytes 589832 | tf_op jit(solution)/shard_map/ppermute | solution.py:90
  15.1 0.7 copy-start.3
  15.1 0.7 copy-start.4
  15.1 0.8 %copy-start.5 = (bf16[96,1024]{1,0:T(8,128)(2,1)}, bf16[96,1024]{1,0:T(8,128)(2,1)S(1)}, u32[]{:S(2)}) copy-start(bf16[96,1024]{1,0:T(8,128)(2,1)S(1)} %collective-permute-done.4.refs_5_) | copy-start | bytes 589828
  15.2 0.8 %copy-start.6 = (bf16[96,1024]{1,0:T(8,128)(2,1)}, bf16[96,1024]{1,0:T(8,128)(2,1)S(1)}, u32[]{:S(2)}) copy-start(bf16[96,1024]{1,0:T(8,128)(2,1)S(1)} %collective-permute-done.2.refs_3_) | copy-start | bytes 589828

commit v4 on v3

--- a/solution.py
+++ b/solution.py
@@ -13,7 +13,7 @@
 PAGE_POSITIONS = 128
 MAX_SLOT_PAGES = 15
 GROUP = QUERY_HEADS // KEY_VALUE_HEADS
-PAGE_BLOCK = 32
+PAGE_BLOCK = 128
 STATS = 128
 NT = (((1,), (1,)), ((), ()))
 NEG = float("-inf")
@@ -298,8 +298,9 @@
         )
 
     copies = []
-    for step in range(1, kv):
-        peer = lax.rem(me_kv + step, kv)
+    order = [*range(kv // 2, kv), *range(1, kv // 2)]
+    for step in order:
+        peer = me_kv ^ step
         partial[step] = project(peer).astype(jnp.bfloat16)
         copy = pltpu.make_async_remote_copy(
             src_ref=partial.at[step],
@@ -312,7 +313,7 @@
         copy.start()
         copies.append(copy)
     result = project(me_kv)
-    for step, copy in enumerate(copies, 1):
+    for step, copy in zip(order, copies):
         copy.wait()
         result = result + parts[step].astype(jnp.float32)
     out_ref[...] = result.astype(jnp.bfloat16)

time: 74.9 us -> 70.1 us (0.936)
  Pallas kernels: 56.7 us -> 52 us
    pallas_call x1, Pallas kernels: 20.3 us -> 16.1 us  [per_device(): pl.pallas_call(attention_kernel, name='attend_pages', out_shape=jax.Shape...]
  transfers between devices with their start and end apart: 7 -> 7, of which waited for: 0 -> 0; matrix products, arithmetic and copies ran while one was open for 14% -> 15% of each run, Pallas kernels for 0% -> 0%
where the time goes in v4:
time: 70.1 us; the launch traced here: 69.6 us
  Pallas kernels  52 us (74%)
  other arithmetic  7.09 us (10%)
  local copies, waits for them, and re-layouts  5.53 us (8%)
  starting transfers between devices  4.81 us (7%)
    pallas_call x1, Pallas kernels, per_device(): pl.pallas_call(functools.partial(finish_kernel, n, kv, entries), name='co...  36 us
    pallas_call x1, Pallas kernels, per_device(): pl.pallas_call(attention_kernel, name='attend_pages', out_shape=jax.Shape...  16.1 us
    ppermute x7, starting transfers between devices, swap(): return lax.ppermute(block, 'req', [(i, i ^ k) for i in range(n)])  4.81 us
    unnamed x15, local copies, waits for them, and re-layouts  2.44 us
  transfers between devices with their start and end apart: 7, of which 0 were waited for; matrix products, arithmetic and copies ran while one was open for 15% of the time, Pallas kernels for 0%

profile of v4, /device:TPU:9, one launch (start us, length us, event | category | flops | bytes accessed | tf_op | source)
XLA Modules:
  0.0 69.6 jit_solution(4282181928297522631)
XLA Ops:
  0.0 2.2 %collective-permute-start.5 = (bf16[96,1024]{1,0:T(8,128)(2,1)}, bf16[96,1024]{1,0:T(8,128)(2,1)S(1)}, u32[]{:S(2)}, u32[]{:S(2)}) collective-permute-start(bf16[96,1024]{1,0:T(8,128)(2,1)} %query_ref.1), channel_id=1, source_target_pairs={{0,6},{1,7},{2,4},{3,5},{4,2},{5,3},{6,0},{7,1},{8,14},{9,15},{10,... | collective-permute-start | bytes 589832 | tf_op jit(solution)/shard_map/ppermute | solution.py:90
  2.2 0.2 collective-permute-start.3
  2.4 0.3 collective-permute-start.1
  2.7 1.5 %collective-permute-start = (bf16[96,1024]{1,0:T(8,128)(2,1)}, bf16[96,1024]{1,0:T(8,128)(2,1)S(1)}, u32[]{:S(2)}, u32[]{:S(2)}) collective-permute-start(bf16[96,1024]{1,0:T(8,128)(2,1)} %query_ref.1), channel_id=1, source_target_pairs={{0,1},{1,0},{2,3},{3,2},{4,5},{5,4},{6,7},{7,6},{8,9},{9,8},{10,11... | collective-permute-start | bytes 589832 | tf_op jit(solution)/shard_map/ppermute | solution.py:90
  4.2 0.7 %and_reduce_fusion = pred[768]{0:T(1024)(128)(4,1)S(1)} fusion(s32[2,768]{1,0:T(2,128)} %param.12), kind=kLoop, calls=%fused_computation.24 | loop fusion | flops 3840 | bytes 3840 | tf_op jit(solution)/shard_map/jit(floor_divide)/and | solution.py:42
  4.9 0.8 %slice_reduce_fusion = (s32[768]{0:T(1024)S(1)}, s32[768]{0:T(1024)S(1)}, s32[768]{0:T(1024)S(1)}, s32[1,768]{1,0:T(1,128)S(1)}, s32[1,768]{1,0:T(1,128)S(1)}) fusion(s32[2,768]{1,0:T(2,128)} %param.12), kind=kLoop, calls=%fused_computation.64 | loop fusion | flops 768 | bytes 21504 | tf_op jit(solution)/shard_map/slice | solution.py:41
  5.7 0.1 and.96
  5.8 0.7 %add_select_fusion.2 = s32[768]{0:T(1024)S(1)} fusion(s32[768]{0:T(1024)} %param.11), kind=kLoop, calls=%fused_computation.33 | loop fusion | flops 6144 | bytes 6144 | tf_op jit(solution)/shard_map/jit(floor_divide)/jit(_where)/select_n | solution.py:30
  6.5 0.1 eq.44
  6.6 0.3 select_reduce_fusion
  6.9 0.1 div.63
  7.0 0.6 convert_reduce_fusion.1
  7.6 0.1 reshape.226
  7.7 0.1 add.128
  7.8 0.7 sub.84
  8.4 0.7 %multiply_add_fusion = (s32[768]{0:T(1024)S(1)}, s32[768]{0:T(1024)S(1)}, s32[768]{0:T(1024)S(1)}, s32[768]{0:T(1024)S(1)}) fusion(s32[768]{0:T(1024)S(1)} %add.128, s32[768]{0:T(1024)S(1)} %get-tuple-element.8, s32[]{:T(128)S(6)} %axis_index.12, s32[768]{0:T(1024)S(1)} %reshape.226, s32[768]{0:T(1024)} %param.11), kind=kLoop, calls=%fused_computation.37 | loop fusion | flops 26880 | bytes 24580 | tf_op jit(solution)/shard_map/add | solution.py:59
  9.2 0.1 dynamic_slice.11
  9.2 0.1 dynamic-slice_bitcast_fusion
  9.3 1.0 %fusion.2 = (s32[96]{0:T(128)S(1)}, s32[96]{0:T(128)S(1)}, s32[96]{0:T(128)S(1)}) fusion(s32[768]{0:T(1024)S(1)} %get-tuple-element.28, s32[768]{0:T(1024)} %param.11, s32[96]{0:T(128)S(1)} %iota_add_fusion, s32[768]{0:T(1024)S(1)} %sub.84), kind=kLoop, calls=%fused_computation.11 | loop fusion | flops 515808 | bytes 10752 | tf_op jit(solution)/shard_map/reduce_sum | solution.py:53
  10.3 0.1 pad_add_fusion.1
  10.3 0.1 select_reduce_fusion.5
  10.5 0.1 fusion.11
  10.6 0.1 pad_add_fusion.3
  10.7 0.9 %convert_reduce_fusion.2 = (s32[384]{0:T(512)S(1)}, s32[384]{0:T(512)S(1)}, s32[384]{0:T(512)}, s32[384]{0:T(512)S(1)}) fusion(s32[192]{0:T(256)S(1)} %select_reduce_fusion.5, s32[192]{0:T(256)S(1)} %add.135, s32[192]{0:T(256)S(1)} %pad_add_fusion.3, s32[192]{0:T(256)S(1)} %get-tuple-element.23, s32[192]{0:T(256)S(1)} %fusion.11), kind=kLoop, calls=%fused_computation.12 | loop fusion | flops 1251840 | bytes 9984 | tf_op jit(solution)/shard_map/reduce_sum | solution.py:75
  11.5 0.6 reshape.229.first_ref
  12.1 0.6 reshape.228.row_ref
  12.7 0.3 select_reduce_fusion.1
  13.0 0.0 collective-permute-done.5.refs_6_
  13.0 0.0 copy-start
  13.0 0.1 collective-permute-start.6
  13.1 0.0 collective-permute-done.3.refs_4_
  13.1 0.0 copy-start.1
  13.1 0.5 collective-permute-start.4
  13.6 0.0 collective-permute-done.1.refs_2_
  13.6 0.0 copy-start.2
  13.6 0.1 collective-permute-start.2
  13.7 0.6 sub.83.row_ref
  14.3 0.8 %reshape.231.col_ref = s32[384,1]{1,0:T(8,128)} reshape(s32[384]{0:T(512)S(1)} %get-tuple-element.16) | data formatting | bytes 3072 | tf_op jit(solution)/shard_map/reshape | solution.py:367
  15.1 0.0 collective-permute-done.refs_1_
  15.1 0.0 copy-start.3
  15.1 0.0 collective-permute-done.6.refs_7_
  15.1 0.0 copy-start.4
  15.1 0.0 collective-permute-done.4.refs_5_
  15.1 0.0 copy-start.5
  15.1 0.0 collective-permute-done.2.refs_3_
  15.2 0.0 copy-start.6
  15.2 0.0 copy-done
  15.2 0.0 copy-done.1
  15.2 0.0 copy-done.2
  15.2 0.6 copy-done.3
  15.8 0.1 copy-done.4
  15.9 0.1 copy-done.5
  15.9 0.1 copy-done.6
  16.0 16.1 %attend_pages.1 = bf16[384,1152]{1,0:T(8,128)(2,1)} custom-call(s32[384]{0:T(512)} %get-tuple-element.15.used_ref, s32[384,1]{1,0:T(8,128)} %reshape.231.col_ref, s32[1,384]{1,0:T(1,128)} %reshape.228.row_ref, s32[1,384]{1,0:T(1,128)} %reshape.229.first_ref, bf16[96,1024]{1,0:T(8,128)(2,1)} %query_ref.1, bf16[96,1024]{1,0:T(8,128)(2,1)} %copy-done.3, ...), custom_call_target="tpu_custom_call" | custom-call | tf_op jit(solution)/shard_map/attend_pages/pallas_call | solution.py:340
  32.1 36.0 %combine_project.1 = bf16[96,1024]{1,0:T(8,128)(2,1)} custom-call(s32[1,384]{1,0:T(1,128)} %sub.83.row_ref, bf16[96,1024]{1,0:T(8,128)(2,1)} %query_ref.1, bf16[2,96,128]{2,1,0:T(8,128)(2,1)} %latest_ref.1, bf16[8,48,1152]{2,1,0:T(8,128)(2,1)} %bitcast.5, bf16[1024,4096]{1,0:T(8,128)(2,1)} %weight_ref.1), custom_call_target="tpu_custom_call" | custom-call | tf_op jit(solution)/shard_map/combine_project/pallas_call | solution.py:376
  68.0 1.6 %copy.11 = bf16[96,1024]{1,0:T(8,128)(2,1)} copy(bf16[96,1024]{1,0:T(8,128)(2,1)} %combine_project.1) | data formatting | bytes 393216
  (9 shorter events, 0.1 us)
Async XLA Ops:
  0.0 13.0 %collective-permute-start.5 = (bf16[96,1024]{1,0:T(8,128)(2,1)}, bf16[96,1024]{1,0:T(8,128)(2,1)S(1)}, u32[]{:S(2)}, u32[]{:S(2)}) collective-permute-start(bf16[96,1024]{1,0:T(8,128)(2,1)} %query_ref.1), channel_id=1, source_target_pairs={{0,6},{1,7},{2,4},{3,5},{4,2},{5,3},{6,0},{7,1},{8,14},{9,15},{10,... | collective-permute-start | bytes 589832 | tf_op jit(solution)/shard_map/ppermute | solution.py:90
  2.2 10.9 %collective-permute-start.3 = (bf16[96,1024]{1,0:T(8,128)(2,1)}, bf16[96,1024]{1,0:T(8,128)(2,1)S(1)}, u32[]{:S(2)}, u32[]{:S(2)}) collective-permute-start(bf16[96,1024]{1,0:T(8,128)(2,1)} %query_ref.1), channel_id=1, source_target_pairs={{0,4},{1,5},{2,6},{3,7},{4,0},{5,1},{6,2},{7,3},{8,12},{9,13},{10,... | collective-permute-start | bytes 589832 | tf_op jit(solution)/shard_map/ppermute | solution.py:90
  2.4 11.2 %collective-permute-start.1 = (bf16[96,1024]{1,0:T(8,128)(2,1)}, bf16[96,1024]{1,0:T(8,128)(2,1)S(1)}, u32[]{:S(2)}, u32[]{:S(2)}) collective-permute-start(bf16[96,1024]{1,0:T(8,128)(2,1)} %query_ref.1), channel_id=1, source_target_pairs={{0,2},{1,3},{2,0},{3,1},{4,6},{5,7},{6,4},{7,5},{8,10},{9,11},{10,... | collective-permute-start | bytes 589832 | tf_op jit(solution)/shard_map/ppermute | solution.py:90
  2.7 12.5 %collective-permute-start = (bf16[96,1024]{1,0:T(8,128)(2,1)}, bf16[96,1024]{1,0:T(8,128)(2,1)S(1)}, u32[]{:S(2)}, u32[]{:S(2)}) collective-permute-start(bf16[96,1024]{1,0:T(8,128)(2,1)} %query_ref.1), channel_id=1, source_target_pairs={{0,1},{1,0},{2,3},{3,2},{4,5},{5,4},{6,7},{7,6},{8,9},{9,8},{10,11... | collective-permute-start | bytes 589832 | tf_op jit(solution)/shard_map/ppermute | solution.py:90
  13.0 2.1 %copy-start = (bf16[96,1024]{1,0:T(8,128)(2,1)}, bf16[96,1024]{1,0:T(8,128)(2,1)S(1)}, u32[]{:S(2)}) copy-start(bf16[96,1024]{1,0:T(8,128)(2,1)S(1)} %collective-permute-done.5.refs_6_) | copy-start | bytes 589828
  13.0 2.1 %collective-permute-start.6 = (bf16[96,1024]{1,0:T(8,128)(2,1)S(1)}, bf16[96,1024]{1,0:T(8,128)(2,1)S(1)}, u32[]{:S(2)}, u32[]{:S(2)}) collective-permute-start(bf16[96,1024]{1,0:T(8,128)(2,1)S(1)} %collective-permute-done.5.refs_6_), channel_id=1, source_target_pairs={{0,1},{1,0},{2,3},{3,2},{4,5},{5,4},{6,7},{7,6},{8,9},{9,8},{10,11... | collective-permute-start | bytes 589832 | tf_op jit(solution)/shard_map/ppermute | solution.py:90
  13.1 2.1 %copy-start.1 = (bf16[96,1024]{1,0:T(8,128)(2,1)}, bf16[96,1024]{1,0:T(8,128)(2,1)S(1)}, u32[]{:S(2)}) copy-start(bf16[96,1024]{1,0:T(8,128)(2,1)S(1)} %collective-permute-done.3.refs_4_) | copy-start | bytes 589828
  13.1 2.0 %collective-permute-start.4 = (bf16[96,1024]{1,0:T(8,128)(2,1)S(1)}, bf16[96,1024]{1,0:T(8,128)(2,1)S(1)}, u32[]{:S(2)}, u32[]{:S(2)}) collective-permute-start(bf16[96,1024]{1,0:T(8,128)(2,1)S(1)} %collective-permute-done.3.refs_4_), channel_id=1, source_target_pairs={{0,1},{1,0},{2,3},{3,2},{4,5},{5,4},{6,7},{7,6},{8,9},{9,8},{10,11... | collective-permute-start | bytes 589832 | tf_op jit(solution)/shard_map/ppermute | solution.py:90
  13.6 1.6 %copy-start.2 = (bf16[96,1024]{1,0:T(8,128)(2,1)}, bf16[96,1024]{1,0:T(8,128)(2,1)S(1)}, u32[]{:S(2)}) copy-start(bf16[96,1024]{1,0:T(8,128)(2,1)S(1)} %collective-permute-done.1.refs_2_) | copy-start | bytes 589828
  13.6 1.5 %collective-permute-start.2 = (bf16[96,1024]{1,0:T(8,128)(2,1)S(1)}, bf16[96,1024]{1,0:T(8,128)(2,1)S(1)}, u32[]{:S(2)}, u32[]{:S(2)}) collective-permute-start(bf16[96,1024]{1,0:T(8,128)(2,1)S(1)} %collective-permute-done.1.refs_2_), channel_id=1, source_target_pairs={{0,1},{1,0},{2,3},{3,2},{4,5},{5,4},{6,7},{7,6},{8,9},{9,8},{10,11... | collective-permute-start | bytes 589832 | tf_op jit(solution)/shard_map/ppermute | solution.py:90
  15.1 0.7 copy-start.3
  15.1 0.7 %copy-start.4 = (bf16[96,1024]{1,0:T(8,128)(2,1)}, bf16[96,1024]{1,0:T(8,128)(2,1)S(1)}, u32[]{:S(2)}) copy-start(bf16[96,1024]{1,0:T(8,128)(2,1)S(1)} %collective-permute-done.6.refs_7_) | copy-start | bytes 589828
  15.1 0.8 %copy-start.5 = (bf16[96,1024]{1,0:T(8,128)(2,1)}, bf16[96,1024]{1,0:T(8,128)(2,1)S(1)}, u32[]{:S(2)}) copy-start(bf16[96,1024]{1,0:T(8,128)(2,1)S(1)} %collective-permute-done.4.refs_5_) | copy-start | bytes 589828
  15.2 0.8 %copy-start.6 = (bf16[96,1024]{1,0:T(8,128)(2,1)}, bf16[96,1024]{1,0:T(8,128)(2,1)S(1)}, u32[]{:S(2)}) copy-start(bf16[96,1024]{1,0:T(8,128)(2,1)S(1)} %collective-permute-done.2.refs_3_) | copy-start | bytes 589828
